TPU v7x, 256 devices: a whole 4x4x8 slice. The times are simulated.
256 devices in a mesh: rows: 64 (over x, z, core), rep: 4 (over y).
Axes of the slice: x: 4, y: 4, z: 8, core: 2. Of those that a mesh axis runs over, the one named last changes fastest.
Arguments:
- gallery: bfloat16 [65536, 1024], P('rows', 'rep'), may hold values from -6 to 6
- neighbours: int32 [65536, 10], P('rows'), may hold values from 0 to 65535, as said below
- queries: bfloat16 [128, 1024], P(None, 'rep'), may hold values from -6 to 6
- listed: int32 [128, 10], replicated, may hold values from 0 to 65535
Outputs:
- augmented: bfloat16 [65536, 1024], P('rows', 'rep')
- first_scores: float32 [128, 65536], P('rep', 'rows')
- final_scores: float32 [128, 65536], P('rep', 'rows')
Inputs may be any that keep to these rules, and one draw needn't show every extreme that they name: `neighbours`: taking the rows in aligned blocks of 1024, the entries of one block name rows of another block at most 64 times and at most 32 distinct rows of it; in every draw one block is named exactly 64 times, at 32 distinct rows, by each other block.
All inputs are finite; a program needn't handle non-finite values.
Results may differ from a plain program's by a relative error of at most 0.017.
Values may be sent and summed in bfloat16 or wider, within the bound.
A program may use at most 64 MiB of HBM per device.

v0:
```python
import jax
import jax.numpy as jnp
from jax import lax
from jax.sharding import PartitionSpec as P

epsilon = 1e-06
logit_scale = 32.0


def sent_to_all(array, axis):
    size = lax.axis_size(axis)
    return lax.all_to_all(
        jnp.broadcast_to(array[None], (size, *array.shape)), axis, 0, 0, tiled=True
    )


def taken_together(array, axis):
    return sent_to_all(array, axis).astype(jnp.float32).sum(axis=0)


def padded_to(lines, size):
    spare = -lines.shape[0] % size
    if not spare:
        return lines
    return jnp.concatenate([lines, jnp.zeros((spare, *lines.shape[1:]), lines.dtype)])


def joined_along(parts, dim):
    lengths = list(parts.shape[1:])
    lengths[dim] *= parts.shape[0]
    return jnp.moveaxis(parts, 0, dim).reshape(lengths)


def collect(array, axis, dim):
    parts = sent_to_all(array, axis)
    return joined_along(parts, dim)


def cut_along(array, dim, size):
    before, after = (array.shape[:dim], array.shape[dim + 1 :])
    return jnp.moveaxis(array.reshape(*before, size, -1, *after), dim, 0)


def sent_and_summed(array, axis, dim):
    size = lax.axis_size(axis)
    parts = lax.all_to_all(cut_along(array, dim, size), axis, 0, 0, tiled=True)
    return jnp.sum(parts, axis=0)


def total_of(array, axes):
    padded = padded_to(array, lax.axis_size(axes))
    whole = collect(sent_and_summed(padded, axes, 0), axes, 0)
    return lax.slice_in_dim(whole, 0, len(array)).reshape(array.shape)


def in_one(arrays, axis):
    ravelled, at, done = (jnp.concatenate([a.reshape(-1) for a in arrays]), 0, [])
    so_far = total_of(ravelled, axis)
    for a in arrays:
        done.append(so_far[at : at + a.size].reshape(a.shape))
        at += a.size
    return tuple(done)


def summed_on_arrival(array, axis, dim):
    parts = cut_along(array, dim, lax.axis_size(axis))
    arrived = lax.all_to_all(parts, axis, split_axis=0, concat_axis=0, tiled=True)
    return arrived.astype(jnp.float32).sum(axis=0)


def side_by_side(arrays, axis, dim, along):
    columns = [a.reshape(*a.shape[:along], -1) for a in arrays]
    both = jnp.concatenate(columns, axis=along)
    result, at, done = (summed_on_arrival(both, axis, dim), 0, [])
    for a, column in zip(arrays, columns):
        share = result[..., at : at + column.shape[along]]
        done.append(share.reshape(*share.shape[:along], *a.shape[along:]))
        at += column.shape[along]
    return tuple(done)


def split_product(selection, source_rows):
    high_part = selection.astype(jnp.bfloat16)
    low_part = (selection - high_part.astype(jnp.float32)).astype(jnp.bfloat16)
    first = jnp.dot(high_part, source_rows, preferred_element_type=jnp.float32)
    return first + jnp.dot(low_part, source_rows, preferred_element_type=jnp.float32)


def local(gallery, neighbours, queries, listed):
    rows_dev, feature_cols = gallery.shape
    link_count = neighbours.shape[1]
    row_groups = lax.axis_size("rows")
    device = lax.axis_index("rows")
    capacity = rows_dev // 16
    owners = neighbours // rows_dev
    offsets = neighbours - owners * rows_dev
    remote = owners != device
    group_iota = jnp.arange(row_groups, dtype=jnp.int32)
    row_iota = jnp.arange(rows_dev, dtype=jnp.int32)
    owner_hot = ((owners[:, :, None] == group_iota[None, None, :]) & remote[:, :, None]).astype(
        jnp.bfloat16
    )
    slot_count = capacity // 2
    slot_iota = jnp.arange(slot_count, dtype=jnp.int32)
    offset_hots = [
        (offsets[:, column, None] == row_iota[None, :]).astype(jnp.bfloat16)
        for column in range(link_count)
    ]
    counted = jnp.zeros((row_groups, rows_dev), jnp.float32)
    for column in range(link_count):
        counted = counted + jnp.einsum(
            "rg,ro->go",
            owner_hot[:, column, :],
            offset_hots[column],
            preferred_element_type=jnp.float32,
        )
    present = counted > 0.5
    earlier = (row_iota[:, None] < row_iota[None, :]).astype(jnp.bfloat16)
    rank_table = jnp.dot(present.astype(jnp.bfloat16), earlier, preferred_element_type=jnp.float32)
    rank_whole = (rank_table + 0.5).astype(jnp.int32)
    chosen = present[:, :, None] & (rank_whole[:, :, None] == slot_iota[None, None, :])
    requests = jnp.sum(jnp.where(chosen, row_iota[None, :, None], 0), axis=1)
    table_narrow = jnp.minimum(rank_table, 255.0).astype(jnp.bfloat16)
    rank_columns = []
    for column in range(link_count):
        spread_rank = jnp.dot(
            owner_hot[:, column, :], table_narrow, preferred_element_type=jnp.float32
        )
        rank_columns.append(jnp.sum(spread_rank * offset_hots[column].astype(jnp.float32), axis=1))
    rank_grid = (jnp.stack(rank_columns, axis=1) + 0.5).astype(jnp.int32)
    slot_total = row_groups * slot_count
    slot_grid = jnp.where(remote, owners * slot_count + rank_grid, slot_total)
    wanted_hot = (
        lax.all_to_all(requests, "rows", split_axis=0, concat_axis=0, tiled=True)[:, :, None]
        == row_iota[None, None, :]
    ).astype(jnp.bfloat16)
    picked = jnp.einsum(
        "gir,rf->gif", wanted_hot, gallery, preferred_element_type=jnp.float32
    ).astype(jnp.bfloat16)
    replies = lax.all_to_all(picked, "rows", split_axis=0, concat_axis=0, tiled=True)
    arrived = replies.reshape(slot_total, feature_cols)
    link_weights = (2.0 * link_count - jnp.arange(link_count, dtype=jnp.float32)) / (
        2.0 * link_count
    )
    piece_rows = 128
    slot_all = jnp.arange(slot_total, dtype=jnp.int32)

    def augment_piece(start):
        near_links = lax.dynamic_slice_in_dim(offsets, start, piece_rows, 0)
        far_links = lax.dynamic_slice_in_dim(slot_grid, start, piece_rows, 0)
        far_mask = lax.dynamic_slice_in_dim(remote, start, piece_rows, 0)
        near_hit = (near_links[:, :, None] == row_iota[None, None, :]) & jnp.logical_not(far_mask)[
            :, :, None
        ]
        near_select = jnp.sum(jnp.where(near_hit, link_weights[None, :, None], 0.0), axis=1)
        own_rows = start + jnp.arange(piece_rows, dtype=jnp.int32)
        near_select = near_select + (own_rows[:, None] == row_iota[None, :]).astype(jnp.float32)
        far_hit = far_links[:, :, None] == slot_all[None, None, :]
        far_select = jnp.sum(jnp.where(far_hit, link_weights[None, :, None], 0.0), axis=1)
        return split_product(near_select, gallery) + split_product(far_select, arrived)

    starts = jnp.arange(rows_dev // piece_rows, dtype=jnp.int32) * piece_rows
    summed = lax.map(augment_piece, starts).reshape(rows_dev, feature_cols)
    augmented = summed.astype(jnp.bfloat16)
    aug_wide = augmented.astype(jnp.float32)
    row_sq_part = jnp.sum(aug_wide * aug_wide, axis=1)
    query_wide = queries.astype(jnp.float32)
    query_sq_part = jnp.sum(query_wide * query_wide, axis=1)
    first_part = jnp.einsum("qd,rd->qr", queries, augmented, preferred_element_type=jnp.float32)
    query_block = queries.shape[0] // lax.axis_size("rep")
    rep_index = lax.axis_index("rep")
    list_owner = listed // rows_dev
    list_offset = listed - list_owner * rows_dev
    is_mine = list_owner == device
    listed_hit = (list_offset[:, :, None] == row_iota[None, None, :]) & is_mine[:, :, None]
    listed_rows = jnp.einsum(
        "qkr,rf->qkf",
        listed_hit.astype(jnp.bfloat16),
        augmented,
        preferred_element_type=jnp.float32,
    )
    first_full, row_sq, query_sq = (
        taken_together(first_part.astype(jnp.bfloat16), "rep").astype(jnp.float32),
        taken_together(row_sq_part.astype(jnp.bfloat16), "rep").astype(jnp.float32),
        taken_together(query_sq_part.astype(jnp.bfloat16), "rep").astype(jnp.float32),
    )
    listed_sq = jnp.sum(jnp.where(listed_hit, row_sq[None, None, :], 0.0), axis=2)
    logits_full = (
        logit_scale
        * first_full
        * lax.rsqrt(query_sq + epsilon)[:, None]
        * lax.rsqrt(row_sq + epsilon)[None, :]
    )
    first_scores = lax.dynamic_slice_in_dim(logits_full, rep_index * query_block, query_block, 0)
    listed_logit = jnp.sum(jnp.where(listed_hit, logits_full[:, None, :], 0.0), axis=2)
    weights = jnp.where(is_mine, jnp.exp(listed_logit), 0.0)
    unit_rows = listed_rows * lax.rsqrt(listed_sq + epsilon)[..., None]
    numer_part = jnp.sum(weights[..., None] * unit_rows, axis=1)
    denom_part = jnp.sum(weights, axis=1)
    numer, denom = in_one((numer_part, denom_part), "rows")
    expanded = query_wide * lax.rsqrt(query_sq + epsilon)[:, None] + numer / denom[:, None]
    expanded_sq_part = jnp.sum(expanded * expanded, axis=1)
    final_part = jnp.einsum(
        "qd,rd->qr", expanded.astype(jnp.bfloat16), augmented, preferred_element_type=jnp.float32
    )
    final_dot, expanded_sq = side_by_side(
        (final_part.astype(jnp.bfloat16), expanded_sq_part.astype(jnp.bfloat16)), "rep", 0, 1
    )
    final_scores = (
        logit_scale
        * final_dot
        * lax.rsqrt(expanded_sq + epsilon)[:, None]
        * lax.rsqrt(row_sq + epsilon)[None, :]
    )
    return (augmented, first_scores, final_scores)


def solution(mesh):
    return jax.shard_map(
        local,
        mesh=mesh,
        in_specs=(P("rows", "rep"), P("rows", None), P(None, "rep"), P()),
        out_specs=(P("rows", "rep"), P("rep", "rows"), P("rep", "rows")),
        check_vma=False,
    )
```

profile of v0, /device:TPU:1, one launch (start us, length us, event | category | flops | bytes accessed | tf_op | source)
XLA Modules:
  0.0 219.8 jit_solution(10231966572628119937)
XLA Ops:
  12.8 3.1 %select_reduce_fusion.2 = s32[64,32]{1,0:T(8,128)} fusion(s32[64,1024]{1,0:T(8,128)S(1)} %add_convert_fusion, pred[64,1024]{1,0:T(8,128)(4,1)S(1)} %fusion.78), kind=kLoop, calls=%fused_computation.30 | loop fusion | flops 8386560 | bytes 335872 | tf_op jit(solution)/shard_map/reduce_sum | solution.py:122
  15.9 13.2 %all-to-all-start = ((s32[64,1,32]{2,1,0:T(1,128)}), s32[64,1,32]{2,1,0:T(1,128)S(1)}, u32[]{:S(2)}, u32[]{:S(2)}) async-start(s32[64,1,32]{2,1,0:T(1,128)} %bitcast.31), calls=%async_computation | async-start | bytes 65536 | tf_op jit(solution)/shard_map/all_to_all | solution.py:134
  31.6 6.6 %all-to-all-done = s32[64,1,32]{2,1,0:T(1,128)S(1)} async-done(((s32[64,1,32]{2,1,0:T(1,128)}), s32[64,1,32]{2,1,0:T(1,128)S(1)}, u32[]{:S(2)}, u32[]{:S(2)}) %all-to-all-start) | async-done | bytes 8224 | tf_op jit(solution)/shard_map/all_to_all | solution.py:134
  38.3 2.5 %fusion.58 = bf16[64,32,256]{2,1,0:T(8,128)(2,1)} fusion(s32[64,32]{1,0:T(8,128)S(1)} %bitcast.123, bf16[1024,256]{1,0:T(8,128)(2,1)S(1)} %copy-done), kind=kOutput, calls=%fused_computation.97 | convolution fusion | flops 1076363264 | bytes 1581056 | tf_op jit(solution)/shard_map/gir,rf->gif/dot_general | solution.py:137
  40.8 4.8 %all-to-all-start.1 = ((bf16[64,32,256]{2,1,0:T(8,128)(2,1)}), bf16[64,32,256]{2,1,0:T(8,128)(2,1)S(1)}, u32[]{:S(2)}, u32[]{:S(2)}) async-start(bf16[64,32,256]{2,1,0:T(8,128)(2,1)} %fusion.58), calls=%async_computation.1 | async-start | bytes 2097152 | tf_op jit(solution)/shard_map/all_to_all | solution.py:140
  52.0 22.1 %all-to-all-done.1 = bf16[64,32,256]{2,1,0:T(8,128)(2,1)S(1)} async-done(((bf16[64,32,256]{2,1,0:T(8,128)(2,1)}), bf16[64,32,256]{2,1,0:T(8,128)(2,1)S(1)}, u32[]{:S(2)}, u32[]{:S(2)}) %all-to-all-start.1) | async-done | bytes 1048608 | tf_op jit(solution)/shard_map/all_to_all | solution.py:140
  74.7 4.2 %all-to-all-start.3 = ((bf16[4,1,128]{2,1,0:T(2,128)(2,1)}), bf16[4,1,128]{2,1,0:T(2,128)(2,1)S(1)}, u32[]{:S(2)}, u32[]{:S(2)}) async-start(bf16[4,1,128]{2,1,0:T(2,128)(2,1)} %broadcast_in_dim.85), calls=%async_computation.3 | async-start | bytes 4096 | tf_op jit(solution)/shard_map/all_to_all | solution.py:12
  78.9 60.0 %while.12 = (s32[]{:T(128)}, bf16[8,128,256]{2,1,0:T(8,128)(2,1)S(1)}, s32[8]{0:T(128)S(1)}, s32[1024,10]{0,1:T(8,128)S(1)}, pred[1024,10]{0,1:T(8,128)(4,1)S(1)...) while((s32[]{:T(128)}, ...), condition=%wide.region_14.15_spmd.clone.clone, body=%wide.region_11.14_spmd.clone.clone.sunk | while | flops 418219424 | bytes 8818211 | solution.py:163
  81.5 1.5 select_reduce_fusion.7
  83.7 1.4 select_reduce_fusion.8
  89.0 1.5 select_reduce_fusion.7
  91.2 1.4 select_reduce_fusion.8
  96.5 1.5 select_reduce_fusion.7
  98.7 1.4 select_reduce_fusion.8
  104.0 1.5 select_reduce_fusion.7
  106.2 1.4 select_reduce_fusion.8
  111.5 1.5 select_reduce_fusion.7
  113.7 1.4 select_reduce_fusion.8
  119.0 1.5 select_reduce_fusion.7
  126.5 1.5 select_reduce_fusion.7
  134.0 1.5 select_reduce_fusion.7
  136.2 1.4 select_reduce_fusion.8
  141.0 4.2 %all-to-all-start.4 = ((bf16[4,2,512]{2,1,0:T(2,128)(2,1)}), bf16[4,2,512]{2,1,0:T(2,128)(2,1)S(1)}, u32[]{:S(2)}, u32[]{:S(2)}) async-start(bf16[4,2,512]{2,1,0:T(2,128)(2,1)} %reshape.144), calls=%async_computation.4 | async-start | bytes 16384 | tf_op jit(solution)/shard_map/all_to_all | solution.py:12
  145.7 3.7 %all-to-all-done.4 = bf16[4,2,512]{2,1,0:T(2,128)(2,1)S(1)} async-done(((bf16[4,2,512]{2,1,0:T(2,128)(2,1)}), bf16[4,2,512]{2,1,0:T(2,128)(2,1)S(1)}, u32[]{:S(2)}, u32[]{:S(2)}) %all-to-all-start.4) | async-done | bytes 8224 | tf_op jit(solution)/shard_map/all_to_all | solution.py:12
  150.5 3.5 %all-to-all-start.2 = ((bf16[4,128,1024]{2,1,0:T(8,128)(2,1)}), bf16[4,128,1024]{2,1,0:T(8,128)(2,1)S(1)}, u32[]{:S(2)}, u32[]{:S(2)}) async-start(bf16[4,128,1024]{2,1,0:T(8,128)(2,1)} %broadcast_in_dim.84), calls=%async_computation.2 | async-start | bytes 2097152 | tf_op jit(solution)/shard_map/all_to_all | solution.py:12
  154.1 12.9 %all-to-all-done.2 = bf16[4,128,1024]{2,1,0:T(8,128)(2,1)S(1)} async-done(((bf16[4,128,1024]{2,1,0:T(8,128)(2,1)}), bf16[4,128,1024]{2,1,0:T(8,128)(2,1)S(1)}, u32[]{:S(2)}, u32[]{:S(2)}) %all-to-all-start.2) | async-done | bytes 1048608 | tf_op jit(solution)/shard_map/all_to_all | solution.py:12
  167.3 2.6 %select_reduce_fusion.3 = (f32[128,10]{0,1:T(8,128)S(1)}, f32[128,10]{0,1:T(8,128)S(1)}) fusion(f32[1024]{0:T(1024)S(1)} %convert_reduce_fusion.2, s32[128,10]{0,1:T(8,128)S(1)} %multiply_subtract_fusion.1, pred[128,10]{0,1:T(8,128)(4,1)S(1)} %fusion.91, f32[128,1024]{1,0:T(8,128)S(1)} %multiply_multiply_fusion), kind=kLoop, calls=%fused_computation.34 | loop fusion | flops 7861760 | bytes 545024 | tf_op jit(solution)/shard_map/reduce_sum | solution.py:187
  169.9 1.5 fusion.65
  171.8 19.1 %all_to_all.51 = f32[64,1,514]{2,1,0:T(1,128)S(1)} all-to-all(f32[64,1,514]{2,1,0:T(1,128)S(1)} %all_to_all.39), channel_id=1, replica_groups=mesh['rows'=64,'rep'=4] {'rows'}, dimensions={0} | all-to-all | bytes 263168 | tf_op jit(solution)/shard_map/all_to_all | solution.py:46
  191.2 15.7 %all_to_all.52 = f32[64,1,514]{2,1,0:T(1,128)S(1)} all-to-all(f32[64,1,514]{2,1,0:T(1,128)S(1)} %broadcast_in_dim.95), channel_id=1, replica_groups=mesh['rows'=64,'rep'=4] {'rows'}, dimensions={0} | all-to-all | bytes 263168 | tf_op jit(solution)/shard_map/all_to_all | solution.py:12
  209.1 3.5 %all-to-all-start.7 = ((bf16[4,32,1025]{2,1,0:T(8,128)(2,1)}), bf16[4,32,1025]{2,1,0:T(8,128)(2,1)S(1)}, u32[]{:S(2)}, u32[]{:S(2)}) async-start(bf16[4,32,1025]{2,1,0:T(8,128)(2,1)} %pad_maximum_fusion), calls=%async_computation.7 | async-start | bytes 589824 | tf_op jit(solution)/shard_map/all_to_all | solution.py:67
  213.2 5.7 %all-to-all-done.7 = bf16[4,32,1025]{2,1,0:T(8,128)(2,1)S(1)} async-done(((bf16[4,32,1025]{2,1,0:T(8,128)(2,1)}), bf16[4,32,1025]{2,1,0:T(8,128)(2,1)S(1)}, u32[]{:S(2)}, u32[]{:S(2)}) %all-to-all-start.7) | async-done | bytes 262432 | tf_op jit(solution)/shard_map/all_to_all | solution.py:67
  (153 shorter events, 53.6 us)
Async XLA Ops:
  15.9 22.4 %all-to-all-start = ((s32[64,1,32]{2,1,0:T(1,128)}), s32[64,1,32]{2,1,0:T(1,128)S(1)}, u32[]{:S(2)}, u32[]{:S(2)}) async-start(s32[64,1,32]{2,1,0:T(1,128)} %bitcast.31), calls=%async_computation | async-start | bytes 65536 | tf_op jit(solution)/shard_map/all_to_all | solution.py:134
  30.8 7.5 %copy-start = (bf16[1024,256]{1,0:T(8,128)(2,1)S(1)}, bf16[1024,256]{1,0:T(8,128)(2,1)}, u32[]{:S(2)}) copy-start(bf16[1024,256]{1,0:T(8,128)(2,1)} %param.6) | copy-start | bytes 1572868
  40.8 33.3 %all-to-all-start.1 = ((bf16[64,32,256]{2,1,0:T(8,128)(2,1)}), bf16[64,32,256]{2,1,0:T(8,128)(2,1)S(1)}, u32[]{:S(2)}, u32[]{:S(2)}) async-start(bf16[64,32,256]{2,1,0:T(8,128)(2,1)} %fusion.58), calls=%async_computation.1 | async-start | bytes 2097152 | tf_op jit(solution)/shard_map/all_to_all | solution.py:140
  50.7 1.0 copy-start.3
  50.8 1.1 copy-start.4
  50.8 1.1 copy-start.2
  74.7 66.3 %all-to-all-start.3 = ((bf16[4,1,128]{2,1,0:T(2,128)(2,1)}), bf16[4,1,128]{2,1,0:T(2,128)(2,1)S(1)}, u32[]{:S(2)}, u32[]{:S(2)}) async-start(bf16[4,1,128]{2,1,0:T(2,128)(2,1)} %broadcast_in_dim.85), calls=%async_computation.3 | async-start | bytes 4096 | tf_op jit(solution)/shard_map/all_to_all | solution.py:12
  138.9 68.7 %copy-start.1 = (bf16[8,128,256]{2,1,0:T(8,128)(2,1)}, bf16[8,128,256]{2,1,0:T(8,128)(2,1)S(1)}, u32[]{:S(2)}) copy-start(bf16[8,128,256]{2,1,0:T(8,128)(2,1)S(1)} %get-tuple-element.66) | copy-start | bytes 1572868
  141.0 8.4 %all-to-all-start.4 = ((bf16[4,2,512]{2,1,0:T(2,128)(2,1)}), bf16[4,2,512]{2,1,0:T(2,128)(2,1)S(1)}, u32[]{:S(2)}, u32[]{:S(2)}) async-start(bf16[4,2,512]{2,1,0:T(2,128)(2,1)} %reshape.144), calls=%async_computation.4 | async-start | bytes 16384 | tf_op jit(solution)/shard_map/all_to_all | solution.py:12
  150.5 16.5 %all-to-all-start.2 = ((bf16[4,128,1024]{2,1,0:T(8,128)(2,1)}), bf16[4,128,1024]{2,1,0:T(8,128)(2,1)S(1)}, u32[]{:S(2)}, u32[]{:S(2)}) async-start(bf16[4,128,1024]{2,1,0:T(8,128)(2,1)} %broadcast_in_dim.84), calls=%async_computation.2 | async-start | bytes 2097152 | tf_op jit(solution)/shard_map/all_to_all | solution.py:12
  209.1 9.9 %all-to-all-start.7 = ((bf16[4,32,1025]{2,1,0:T(8,128)(2,1)}), bf16[4,32,1025]{2,1,0:T(8,128)(2,1)S(1)}, u32[]{:S(2)}, u32[]{:S(2)}) async-start(bf16[4,32,1025]{2,1,0:T(8,128)(2,1)} %pad_maximum_fusion), calls=%async_computation.7 | async-start | bytes 589824 | tf_op jit(solution)/shard_map/all_to_all | solution.py:67
where the time goes:
time: 221 us; the launch traced here: 220 us
  waiting for transfers between devices  51.1 us (23%)
  other arithmetic  40.7 us (18%)
  blocking collectives  34.8 us (16%)
  starting transfers between devices  33.3 us (15%)
  matrix products  32.7 us (15%)
  loops' own time  16.1 us (7%)
  local copies, waits for them, and re-layouts  10.1 us (5%)
    all_to_all x1, waiting for transfers between devices, local(): lax.all_to_all(picked, 'rows', split_axis=0, concat_axis=0, tiled=True)  22.1 us
    all_to_all x1, blocking collectives, sent_and_summed(): parts = lax.all_to_all(cut_along(array, dim, size), axis, 0, 0, tiled=True)  19.1 us
    all_to_all x3, waiting for transfers between devices, sent_to_all(): lax.all_to_all(jnp.broadcast_to(array[None], (size, *array.shape)), axis,...  16.6 us
    another operation x1, loops' own time, local(): summed = lax.map(augment_piece, starts).reshape(rows_dev, feature_cols)  16.1 us
    all_to_all x1, blocking collectives, sent_to_all(): lax.all_to_all(jnp.broadcast_to(array[None], (size, *array.shape)), axis,...  15.7 us
    all_to_all x1, starting transfers between devices, local(): lax.all_to_all(requests, 'rows', split_axis=0, concat_axis=0, tiled=True)  13.2 us
    all_to_all x3, starting transfers between devices, sent_to_all(): lax.all_to_all(jnp.broadcast_to(array[None], (size, *array.shape)), axis,...  11.9 us
    reduce_sum x8, other arithmetic, augment_piece(): jnp.sum(jnp.where(far_hit, link_weights[None, :, None], 0.0), axis=1)  11.8 us
  transfers between devices with their start and end apart: 6, of which 5 were waited for; matrix products, arithmetic and copies ran while one was open for 25% of the time, Pallas kernels for 0%

commit v1 on v0

v1 whole, which is shorter than its diff:
```python
import jax
import jax.numpy as jnp
from jax import lax
from jax.experimental import pallas as pl
from jax.experimental.pallas import tpu as pltpu
from jax.sharding import PartitionSpec as P

epsilon = 1e-06
logit_scale = 32.0
MESH = pl.DeviceIdType.MESH
f32, bf16, i32 = jnp.float32, jnp.bfloat16, jnp.int32

ROWS = 1024
COLS = 256
LINKS = 10
SLOTS = 32
XS, ZS, CS, YS = 4, 8, 2, 4
BLOCKS = XS * ZS * CS
QUERIES = 128
SHARE = QUERIES // YS
GROUP = 8
GROUPS = BLOCKS // GROUP


def split_offset(d):
    return d // (ZS * CS), (d // CS) % ZS, d % CS


def mirrored(d):
    dx, dz, dc = split_offset(d)
    return ((XS - dx) % XS) * (ZS * CS) + ((ZS - dz) % ZS) * CS + dc


def iota(shape, dim):
    return lax.broadcasted_iota(i32, shape, dim)


def dot(a, b, contract=((1,), (0,))):
    return lax.dot_general(a, b, (contract, ((), ())), preferred_element_type=f32)


def one_hot(mask):
    return jnp.where(mask, 1.0, 0.0).astype(bf16)


def wait_for(buffer, sem):
    pltpu.make_async_copy(buffer, buffer, sem).wait()


def kernel(
    gal_ref, nbt_ref, q_ref, lst_ref,
    aug_ref, first_ref, final_ref,
    nbb, cums, counts, req_out, req_in, cols, sel, picked, arrived, pick, acc, augt, rows_t, lsb,
    lsq_out, lsq_in, ft_out, ft_in, rsq_out, rsq_in,
    part, part_in, half, half_in, piece, whole, esq_out, esq_in, fp_out, fp_in, esq_col,
    send_req, recv_req, send_rep, recv_rep, send_y, recv_y, send_p, recv_p, send_e, recv_e,
):
    me = lax.axis_index("rows")
    my_y = lax.axis_index("rep")
    mx, mz, mc = me // (ZS * CS), (me // CS) % ZS, me % CS

    def peer(d):
        dx, dz, dc = split_offset(d)
        return ((mx + dx) % XS) * (ZS * CS) + ((mz + dz) % ZS) * CS + (mc + dc) % CS

    def send(src, dst, s_sem, r_sem, target):
        pltpu.make_async_remote_copy(
            src_ref=src, dst_ref=dst, send_sem=s_sem, recv_sem=r_sem,
            device_id=target, device_id_type=MESH,
        ).start()

    barrier = pltpu.get_barrier_semaphore()

    def greet(d, carry):
        pl.semaphore_signal(barrier, inc=1, device_id={"rows": peer(d)}, device_id_type=MESH)
        return carry

    lax.fori_loop(1, BLOCKS, greet, 0)
    for e in range(1, YS):
        pl.semaphore_signal(
            barrier, inc=1, device_id={"rep": (my_y + e) % YS}, device_id_type=MESH
        )

    wide = jnp.concatenate(
        [nbt_ref[...].astype(f32), jnp.zeros((128 - LINKS, ROWS), f32)], axis=0
    )
    for block in range(ROWS // 128):
        turned = jnp.transpose(wide[:, block * 128 : (block + 1) * 128]).astype(i32)
        for k in range(LINKS):
            nbb[k, block * 128 : (block + 1) * 128, :] = jnp.broadcast_to(
                turned[:, k : k + 1], (128, 128)
            )

    cums[...] = jnp.zeros_like(cums)

    def count_link(k, carry):
        row = nbt_ref[pl.ds(k, 1), :]
        total = jnp.zeros((256, 256), f32)
        for quarter in range(4):
            span = slice(quarter * 256, (quarter + 1) * 256)
            low = one_hot(iota((256, 256), 0) == (row[:, span] & 255))
            column = nbb[k, span, :] >> 8
            high = jnp.concatenate(
                [one_hot(iota((256, 128), 1) == column), one_hot(iota((256, 128), 1) + 128 == column)],
                axis=1,
            )
            total = total + dot(low, high)
        cums[...] += total
        return carry

    lax.fori_loop(0, LINKS, count_link, 0)

    def relative(high):
        block = high >> 2
        x, z, c = block >> 4, (block >> 1) & 7, block & 1
        return (((x - mx) & 3) << 4) | (((z - mz) & 7) << 1) | ((c - mc) & 1)

    high_row = iota((256, 256), 1)
    rel_row = relative(high_row)
    named = one_hot((cums[...] > 0.5) & (rel_row != 0))
    up_to = one_hot(iota((256, 256), 1) <= iota((256, 256), 0))
    earlier = one_hot(
        ((iota((256, 256), 0) >> 2) == (iota((256, 256), 1) >> 2))
        & (iota((256, 256), 0) < iota((256, 256), 1))
    )
    before = dot(jnp.ones((256, 256), bf16), named).astype(bf16)
    cums[...] = dot(up_to, named) + dot(before, earlier)
    for s in range(SLOTS):
        counts[pl.ds(s, 1), :] = jnp.sum(
            jnp.where(cums[...] <= float(s), 1.0, 0.0), axis=0, keepdims=True
        )
    count = jnp.concatenate([counts[...].astype(bf16)] * 4, axis=0)
    to_row = one_hot(iota((BLOCKS, 256), 0) == relative(iota((BLOCKS, 256), 1)))
    asked = dot(to_row, count, ((1,), (1,)))
    for d in range(BLOCKS):
        req_out[d] = asked[d : d + 1, :]

    pl.semaphore_wait(barrier, BLOCKS - 1 + YS - 1)

    def ask(d, carry):
        send(req_out.at[d], req_in.at[mirrored(d)], send_req, recv_req, {"rows": peer(d)})
        return carry

    lax.fori_loop(1, BLOCKS, ask, 0)

    quarter_of = (relative(iota((128, 256), 1)) & 3) == (iota((128, 256), 0) >> 5)
    four = jnp.where(quarter_of, count.astype(f32), 0.0).astype(bf16)
    chunks = BLOCKS * SLOTS // 128
    to_chunk = one_hot(iota((chunks, 256), 0) == (relative(iota((chunks, 256), 1)) >> 2))
    offset = dot(to_chunk, four, ((1,), (1,))).astype(i32)
    rel = iota((chunks, 128), 0) * 4 + (iota((chunks, 128), 1) >> 5)
    owner = (
        (((rel >> 4) + mx) & 3) * (ZS * CS) + ((((rel >> 1) & 7) + mz) & 7) * CS + ((rel + mc) & 1)
    )
    far_ids = jnp.where(offset < ROWS, owner * ROWS + offset, -1)
    near_ids = me * ROWS + iota((ROWS // 128, 128), 0) * 128 + iota((ROWS // 128, 128), 1)
    for c in range(ROWS // 128):
        cols[c] = jnp.broadcast_to(near_ids[c : c + 1, :], (8, 128))
    for c in range(chunks):
        cols[ROWS // 128 + c] = jnp.broadcast_to(far_ids[c : c + 1, :], (8, 128))
    arrived[0] = jnp.zeros((SLOTS, COLS), bf16)

    wait_for(req_in.at[pl.ds(1, BLOCKS - 1)], recv_req)
    wanted = jnp.concatenate(
        [req_in[d] if d else jnp.full((1, 128), float(ROWS), f32) for d in range(BLOCKS)]
        + [jnp.zeros((128 - BLOCKS, 128), f32)],
        axis=0,
    )
    wanted = jnp.transpose(wanted).astype(i32)
    for group in range(GROUPS):
        for j in range(GROUP):
            d = group * GROUP + j
            place = wanted[0:SLOTS, d : d + 1]
            pick[j * SLOTS : (j + 1) * SLOTS, :] = one_hot(iota((SLOTS, ROWS), 1) == place)
        taken = dot(pick[...], gal_ref[...]).astype(bf16)
        for j in range(GROUP):
            picked[group * GROUP + j] = taken[j * SLOTS : (j + 1) * SLOTS, :]
        for j in range(GROUP):
            d = group * GROUP + j
            if d:
                send(
                    picked.at[d], arrived.at[mirrored(d)], send_rep,
                    recv_rep.at[mirrored(d) // GROUP], {"rows": peer(d)},
                )

    def choose(block, carry):
        at = pl.multiple_of(block * 16, 16)
        ids = [nbb[k, pl.ds(at, 16), :] for k in range(LINKS)]
        for c in range(ROWS // 128 + chunks):
            column = cols[c]
            column = jnp.concatenate([column, column], axis=0)
            total = jnp.zeros((16, 128), f32)
            for k in range(LINKS):
                total = total + jnp.where(ids[k] == column, float(2 * LINKS - k), 0.0)
            sel[pl.ds(at, 16), c * 128 : (c + 1) * 128] = total.astype(bf16)
        return carry

    lax.fori_loop(0, ROWS // 16, choose, 0)
    acc[...] = float(2 * LINKS) * gal_ref[...].astype(f32)
    acc[...] += dot(sel[:, :ROWS], gal_ref[...])

    owned = lst_ref[...] >> 10
    inside = jnp.where(owned == me, lst_ref[...] & (ROWS - 1), -1)
    for k in range(LINKS):
        lsb[:, k * 128 : (k + 1) * 128] = one_hot(
            iota((ROWS, 128), 0) == inside[k : k + 1, :]
        )
    q_t = jnp.transpose(q_ref[...].astype(f32))
    query_sq = jnp.sum(q_t * q_t, axis=0, keepdims=True)

    for group in range(GROUPS):
        first_slot = 1 if group == 0 else group * GROUP
        last_slot = (group + 1) * GROUP
        wait_for(arrived.at[pl.ds(first_slot, last_slot - first_slot)], recv_rep.at[group])
        begin = ROWS + group * GROUP * SLOTS
        rows = arrived[group * GROUP : last_slot].reshape(GROUP * SLOTS, COLS)
        acc[...] += dot(sel[:, begin : begin + GROUP * SLOTS], rows)

    augmented = (acc[...] * (1.0 / (2 * LINKS))).astype(bf16)
    aug_ref[...] = augmented
    aug_t = jnp.transpose(augmented.astype(f32))
    augt[...] = aug_t.astype(bf16)

    def y_peer(e):
        return {"rep": (my_y + e) % YS}

    lsq_out[...] = jnp.zeros_like(lsq_out)
    for k in range(0, LINKS, 2):
        pair = dot(augt[...], lsb[:, k * 128 : (k + 2) * 128])
        rows_t[:, k * 128 : (k + 2) * 128] = pair
        for j in range(2):
            rows = pair[:, j * 128 : (j + 1) * 128]
            lsq_out[k + j : k + j + 1, :] = jnp.sum(rows * q_t, axis=0, keepdims=True)
            lsq_out[LINKS + k + j : LINKS + k + j + 1, :] = jnp.sum(
                rows * rows, axis=0, keepdims=True
            )
    lsq_out[2 * LINKS : 2 * LINKS + 1, :] = query_sq
    for e in (2, 1, 3):
        send(lsq_out, lsq_in.at[YS - e], send_y.at[0], recv_y.at[0], y_peer(e))

    row_sq = jnp.sum(aug_t * aug_t, axis=0, keepdims=True)
    rsq_out[...] = row_sq
    first = dot(q_ref[...], augt[...])
    for y in range(YS):
        ft_out[y] = first[y * SHARE : (y + 1) * SHARE, :].astype(bf16)
    for e in (2, 1, 3):
        send(rsq_out, rsq_in.at[YS - e], send_y.at[1], recv_y.at[1], y_peer(e))
        send(ft_out.at[(my_y + e) % YS], ft_in.at[YS - e], send_y.at[2], recv_y.at[2], y_peer(e))

    wait_for(lsq_in.at[pl.ds(1, YS - 1)], recv_y.at[0])
    sums = lsq_out[...] + lsq_in[1] + lsq_in[2] + lsq_in[3]
    q_scale = lax.rsqrt(sums[2 * LINKS : 2 * LINKS + 1, :] + epsilon)
    numer = jnp.zeros((COLS, QUERIES), f32)
    denom = jnp.zeros((1, QUERIES), f32)
    for k in range(LINKS):
        unit = lax.rsqrt(sums[LINKS + k : LINKS + k + 1, :] + epsilon)
        logit = logit_scale * sums[k : k + 1, :] * q_scale * unit
        weight = jnp.where(inside[k : k + 1, :] >= 0, jnp.exp(logit), 0.0)
        denom = denom + weight
        numer = numer + rows_t[:, k * 128 : (k + 1) * 128] * (weight * unit)

    def two_rows(total):
        high = total.astype(bf16).astype(f32)
        at = iota((16, QUERIES), 0)
        return jnp.where(at == 0, high, jnp.where(at == 1, total - high, 0.0)).astype(bf16)

    slice_rows = COLS // (XS * CS)
    tail = two_rows(denom)
    for i in range(XS * CS):
        part[i, 0:slice_rows] = numer[i * slice_rows : (i + 1) * slice_rows, :].astype(bf16)
        part[i, slice_rows:] = tail
    mine = mx * CS + mc

    def near(e):
        ex, ec = e // CS, e % CS
        return (mx + ex) % XS, (mc + ec) % CS, ((XS - ex) % XS) * CS + ec

    order = (4, 5, 2, 3, 6, 7, 1)
    for e in order:
        px, pc, back = near(e)
        send(
            part.at[px * CS + pc], part_in.at[back], send_p.at[0], recv_p.at[0],
            {"rows": px * (ZS * CS) + mz * CS + pc},
        )
    wait_for(part_in.at[pl.ds(1, XS * CS - 1)], recv_p.at[0])
    so_far = part[mine].astype(f32)
    for e in range(1, XS * CS):
        so_far = so_far + part_in[e].astype(f32)
    half[0:slice_rows] = so_far[0:slice_rows].astype(bf16)
    half[slice_rows:] = two_rows(so_far[slice_rows : slice_rows + 1] + so_far[slice_rows + 1 : slice_rows + 2])
    for e in (4, 3, 5, 2, 6, 1, 7):
        send(
            half, half_in.at[ZS - e], send_p.at[1], recv_p.at[1],
            {"rows": mx * (ZS * CS) + ((mz + e) % ZS) * CS + mc},
        )

    wait_for(rsq_in.at[pl.ds(1, YS - 1)], recv_y.at[1])
    wait_for(ft_in.at[pl.ds(1, YS - 1)], recv_y.at[2])
    row_scale = lax.rsqrt(rsq_out[...] + rsq_in[1] + rsq_in[2] + rsq_in[3] + epsilon)
    q_col = jnp.transpose(jnp.broadcast_to(q_scale * logit_scale, (QUERIES, QUERIES)))
    esq_col[...] = q_col
    mine_q = pl.ds(pl.multiple_of(my_y * SHARE, SHARE), SHARE)
    q_mine = esq_col[mine_q, 0:1]
    total = ft_out[my_y].astype(f32)
    for e in range(1, YS):
        total = total + ft_in[e].astype(f32)
    first_ref[...] = total * q_mine * row_scale

    wait_for(half_in.at[pl.ds(1, ZS - 1)], recv_p.at[1])
    so_far = half[...].astype(f32)
    for e in range(1, ZS):
        so_far = so_far + half_in[e].astype(f32)
    denom = so_far[slice_rows : slice_rows + 1] + so_far[slice_rows + 1 : slice_rows + 2]
    piece[...] = (so_far[0:slice_rows] / denom).astype(bf16)
    for e in order:
        px, pc, back = near(e)
        send(
            piece, whole.at[mine], send_p.at[2], recv_p.at[2],
            {"rows": px * (ZS * CS) + mz * CS + pc},
        )
    wait_for(whole.at[pl.ds(1, XS * CS - 1)], recv_p.at[2])
    whole[mine] = piece[...]

    expanded_t = q_t * q_scale + whole[...].reshape(COLS, QUERIES).astype(f32)
    esq_out[...] = jnp.sum(expanded_t * expanded_t, axis=0, keepdims=True)
    expanded = jnp.transpose(expanded_t).astype(bf16)
    final = dot(expanded, augt[...])
    for y in range(YS):
        fp_out[y] = final[y * SHARE : (y + 1) * SHARE, :].astype(bf16)
    for e in (2, 1, 3):
        send(esq_out, esq_in.at[YS - e], send_e.at[0], recv_e.at[0], y_peer(e))
        send(fp_out.at[(my_y + e) % YS], fp_in.at[YS - e], send_e.at[1], recv_e.at[1], y_peer(e))
    wait_for(esq_in.at[pl.ds(1, YS - 1)], recv_e.at[0])
    e_scale = lax.rsqrt(esq_out[...] + esq_in[1] + esq_in[2] + esq_in[3] + epsilon)
    esq_col[...] = jnp.transpose(jnp.broadcast_to(e_scale * logit_scale, (QUERIES, QUERIES)))
    e_mine = esq_col[mine_q, 0:1]
    wait_for(fp_in.at[pl.ds(1, YS - 1)], recv_e.at[1])
    total = fp_out[my_y].astype(f32)
    for e in range(1, YS):
        total = total + fp_in[e].astype(f32)
    final_ref[...] = total * e_mine * row_scale

    wait_for(req_out.at[pl.ds(1, BLOCKS - 1)], send_req)
    wait_for(picked.at[pl.ds(1, BLOCKS - 1)], send_rep)
    wait_for(lsq_in.at[pl.ds(1, YS - 1)], send_y.at[0])
    wait_for(rsq_in.at[pl.ds(1, YS - 1)], send_y.at[1])
    wait_for(ft_in.at[pl.ds(1, YS - 1)], send_y.at[2])
    wait_for(part_in.at[pl.ds(1, XS * CS - 1)], send_p.at[0])
    wait_for(half_in.at[pl.ds(1, ZS - 1)], send_p.at[1])
    wait_for(whole.at[pl.ds(1, XS * CS - 1)], send_p.at[2])
    wait_for(esq_in.at[pl.ds(1, YS - 1)], send_e.at[0])
    wait_for(fp_in.at[pl.ds(1, YS - 1)], send_e.at[1])


def local(gallery, neighbours, queries, listed):
    vmem = pl.BlockSpec(memory_space=pltpu.VMEM)
    slice_rows = COLS // (XS * CS)
    columns = ROWS + BLOCKS * SLOTS
    dma = pltpu.SemaphoreType.DMA
    return pl.pallas_call(
        kernel,
        out_shape=(
            jax.ShapeDtypeStruct((ROWS, COLS), bf16),
            jax.ShapeDtypeStruct((SHARE, ROWS), f32),
            jax.ShapeDtypeStruct((SHARE, ROWS), f32),
        ),
        in_specs=[vmem] * 4,
        out_specs=(vmem,) * 3,
        scratch_shapes=[
            pltpu.VMEM((LINKS, ROWS, 128), i32),
            pltpu.VMEM((256, 256), f32),
            pltpu.VMEM((SLOTS, 256), f32),
            pltpu.VMEM((BLOCKS, 1, 128), f32),
            pltpu.VMEM((BLOCKS, 1, 128), f32),
            pltpu.VMEM((columns // 128, 8, 128), i32),
            pltpu.VMEM((ROWS, columns), bf16),
            pltpu.VMEM((BLOCKS, SLOTS, COLS), bf16),
            pltpu.VMEM((BLOCKS, SLOTS, COLS), bf16),
            pltpu.VMEM((GROUP * SLOTS, ROWS), bf16),
            pltpu.VMEM((ROWS, COLS), f32),
            pltpu.VMEM((COLS, ROWS), bf16),
            pltpu.VMEM((COLS, LINKS * QUERIES), f32),
            pltpu.VMEM((ROWS, LINKS * QUERIES), bf16),
            pltpu.VMEM((24, QUERIES), f32),
            pltpu.VMEM((YS, 24, QUERIES), f32),
            pltpu.VMEM((YS, SHARE, ROWS), bf16),
            pltpu.VMEM((YS, SHARE, ROWS), bf16),
            pltpu.VMEM((1, ROWS), f32),
            pltpu.VMEM((YS, 1, ROWS), f32),
            pltpu.VMEM((XS * CS, slice_rows + 16, QUERIES), bf16),
            pltpu.VMEM((XS * CS, slice_rows + 16, QUERIES), bf16),
            pltpu.VMEM((slice_rows + 16, QUERIES), bf16),
            pltpu.VMEM((ZS, slice_rows + 16, QUERIES), bf16),
            pltpu.VMEM((slice_rows, QUERIES), bf16),
            pltpu.VMEM((XS * CS, slice_rows, QUERIES), bf16),
            pltpu.VMEM((1, QUERIES), f32),
            pltpu.VMEM((YS, 1, QUERIES), f32),
            pltpu.VMEM((YS, SHARE, ROWS), bf16),
            pltpu.VMEM((YS, SHARE, ROWS), bf16),
            pltpu.VMEM((QUERIES, QUERIES), f32),
            dma, dma, dma, dma((GROUPS,)), dma((3,)), dma((3,)), dma((3,)), dma((3,)), dma((2,)), dma((2,)),
        ],
        compiler_params=pltpu.CompilerParams(
            collective_id=0, has_side_effects=True, vmem_limit_bytes=60 * 1024 * 1024
        ),
        name="expand",
    )(gallery, neighbours.T, queries, listed.T)


def solution(mesh):
    return jax.shard_map(
        local,
        mesh=mesh,
        in_specs=(P("rows", "rep"), P("rows", None), P(None, "rep"), P()),
        out_specs=(P("rows", "rep"), P("rep", "rows"), P("rep", "rows")),
        check_vma=False,
    )
```

time: 221 us -> 79.7 us (0.36)
  Pallas kernels: 0 us -> 75.4 us
  waiting for transfers between devices: 51.1 us -> 0 us
  other arithmetic: 40.7 us -> 0 us
  blocking collectives: 34.8 us -> 0 us
  starting transfers between devices: 33.3 us -> 0 us
  matrix products: 32.7 us -> 0 us
  loops' own time: 16.1 us -> 0 us
  local copies, waits for them, and re-layouts: 10.1 us -> 3.51 us
    pallas_call x0 -> x1, Pallas kernels: none -> 75.4 us  [local(): pl.pallas_call(kernel, out_shape=(jax.ShapeDtypeStruct((ROWS, COLS), bf16...]
    all_to_all x6 -> x0, waiting for transfers between devices: 51.1 us -> none  [the longest x1 22.1 us: local(): lax.all_to_all(picked, 'rows', split_axis=0, concat_axis=0, tiled=True)]
    all_to_all x2 -> x0, blocking collectives: 34.8 us -> none  [the longest x1 19.1 us: sent_and_summed(): parts = lax.all_to_all(cut_along(array, dim, size), axis, 0, 0, tiled=True)]
    all_to_all x6 -> x0, starting transfers between devices: 33.3 us -> none  [the longest x1 13.2 us: local(): lax.all_to_all(requests, 'rows', split_axis=0, concat_axis=0, tiled=True)]
    dot_general x57 -> x0, matrix products: 32.7 us -> none  [the longest x10 9.41 us: local(): jnp.einsum('rg,ro->go', owner_hot[:, column, :], offset_hots[column], pre...]
    reduce_sum x27 -> x0, other arithmetic: 29.5 us -> none  [the longest x8 11.8 us: augment_piece(): jnp.sum(jnp.where(far_hit, link_weights[None, :, None], 0.0), axis=1)]
    another operation x1 -> x0, loops' own time: 16.1 us -> none  [local(): summed = lax.map(augment_piece, starts).reshape(rows_dev, feature_cols)]
    dynamic_slice x17 -> x0, local copies, waits for them, and re-layouts: 5.99 us -> none  [the longest x8 4.69 us: local(): summed = lax.map(augment_piece, starts).reshape(rows_dev, feature_cols)]
  transfers between devices with their start and end apart: 6 -> 0, of which waited for: 5 -> 0; matrix products, arithmetic and copies ran while one was open for 25% -> 0% of each run, Pallas kernels for 0% -> 0%
where the time goes in v1:
time: 79.7 us; the launch traced here: 79.6 us
  Pallas kernels  75.4 us (95%)
  local copies, waits for them, and re-layouts  3.51 us (4%)
    pallas_call x1, Pallas kernels, local(): pl.pallas_call(kernel, out_shape=(jax.ShapeDtypeStruct((ROWS, COLS), bf16...  75.4 us
    unnamed x7, local copies, waits for them, and re-layouts  3.51 us

profile of v1, /device:TPU:1, one launch (start us, length us, event | category | flops | bytes accessed | tf_op | source)
XLA Modules:
  0.0 79.6 jit_solution(846556151911719008)
XLA Ops:
  0.6 75.4 %expand.1 = (bf16[1024,256]{1,0:T(8,128)(2,1)}, f32[32,1024]{1,0:T(8,128)}, f32[32,1024]{1,0:T(8,128)}) custom-call(bf16[1024,256]{1,0:T(8,128)(2,1)} %gal_ref.1, s32[10,1024]{1,0:T(8,128)} %bitcast.2, bf16[128,256]{1,0:T(8,128)(2,1)} %q_ref.1, s32[10,128]{1,0:T(8,128)} %bitcast.3), custom_call_target="tpu_custom_call" | custom-call | tf_op jit(solution)/shard_map/expand/pallas_call | solution.py:360
  76.0 0.0 copy-start.1
  76.0 1.9 %copy.10 = bf16[1024,256]{1,0:T(8,128)(2,1)} copy(bf16[1024,256]{1,0:T(8,128)(2,1)} %get-tuple-element.6) | data formatting | bytes 1048576
  78.0 0.0 copy-done.1
  78.0 0.0 copy-start
  78.0 0.7 copy.11
  78.6 0.3 copy-done
  78.9 0.7 copy.12
Async XLA Ops:
  76.0 1.9 %copy-start.1 = (f32[32,1024]{1,0:T(8,128)S(1)}, f32[32,1024]{1,0:T(8,128)}, u32[]{:S(2)}) copy-start(f32[32,1024]{1,0:T(8,128)} %get-tuple-element.7) | copy-start | bytes 393220
  78.0 1.0 %copy-start = (f32[32,1024]{1,0:T(8,128)S(1)}, f32[32,1024]{1,0:T(8,128)}, u32[]{:S(2)}) copy-start(f32[32,1024]{1,0:T(8,128)} %get-tuple-element.8) | copy-start | bytes 393220

commit v2 on v1

--- a/solution.py
+++ b/solution.py
@@ -20,15 +20,23 @@
 SHARE = QUERIES // YS
 GROUP = 8
 GROUPS = BLOCKS // GROUP
-
-
-def split_offset(d):
-    return d // (ZS * CS), (d // CS) % ZS, d % CS
-
-
-def mirrored(d):
-    dx, dz, dc = split_offset(d)
-    return ((XS - dx) % XS) * (ZS * CS) + ((ZS - dz) % ZS) * CS + dc
+TAIL = 8
+
+
+FAR_FIRST = (4, 3, 5, 2, 6, 1, 7, 0)
+OWN = (ZS - 1) * XS * CS
+
+
+def split_offset(slot):
+    return (slot // CS) % XS, FAR_FIRST[slot // (XS * CS)], slot % CS
+
+
+def mirrored(slot):
+    dx, dz, dc = split_offset(slot)
+    return FAR_FIRST.index((ZS - dz) % ZS) * (XS * CS) + ((XS - dx) % XS) * CS + dc
+
+
+OTHERS = tuple(slot for slot in range(BLOCKS) if slot != OWN)
 
 
 def iota(shape, dim):
@@ -43,25 +51,33 @@
     return jnp.where(mask, 1.0, 0.0).astype(bf16)
 
 
+def narrow_hot(mask):
+    return jnp.where(mask, jnp.ones((), bf16), jnp.zeros((), bf16))
+
+
 def wait_for(buffer, sem):
     pltpu.make_async_copy(buffer, buffer, sem).wait()
 
 
 def kernel(
-    gal_ref, nbt_ref, q_ref, lst_ref,
+    gal_far, nbt_far, q_far, lst_far,
     aug_ref, first_ref, final_ref,
-    nbb, cums, counts, req_out, req_in, cols, sel, picked, arrived, pick, acc, augt, rows_t, lsb,
+    gal_ref, nbt_ref, q_ref, lst_ref, nbb, cums, counts, req_out, req_in, cols, sel, picked, arrived, pick, acc, augt, rows_t, lsb,
     lsq_out, lsq_in, ft_out, ft_in, rsq_out, rsq_in,
     part, part_in, half, half_in, piece, whole, esq_out, esq_in, fp_out, fp_in, esq_col,
-    send_req, recv_req, send_rep, recv_rep, send_y, recv_y, send_p, recv_p, send_e, recv_e,
+    sem_in, send_req, recv_req, send_rep, recv_rep, send_y, recv_y, send_p, recv_p, send_e, recv_e,
 ):
     me = lax.axis_index("rows")
     my_y = lax.axis_index("rep")
     mx, mz, mc = me // (ZS * CS), (me // CS) % ZS, me % CS
 
-    def peer(d):
-        dx, dz, dc = split_offset(d)
-        return ((mx + dx) % XS) * (ZS * CS) + ((mz + dz) % ZS) * CS + (mc + dc) % CS
+    at_x = [((mx + dx) % XS) * (ZS * CS) for dx in range(XS)]
+    at_z = [((mz + dz) % ZS) * CS for dz in range(ZS)]
+    at_c = [(mc + dc) % CS for dc in range(CS)]
+
+    def peer(slot):
+        dx, dz, dc = split_offset(slot)
+        return {"rows": at_x[dx] + at_z[dz] + at_c[dc]}
 
     def send(src, dst, s_sem, r_sem, target):
         pltpu.make_async_remote_copy(
@@ -69,17 +85,67 @@
             device_id=target, device_id_type=MESH,
         ).start()
 
+    pairs = ((nbt_far, nbt_ref), (gal_far, gal_ref), (q_far, q_ref), (lst_far, lst_ref))
+    bring = [pltpu.make_async_copy(a, b, sem_in.at[i]) for i, (a, b) in enumerate(pairs)]
+    for copy in bring:
+        copy.start()
     barrier = pltpu.get_barrier_semaphore()
 
-    def greet(d, carry):
-        pl.semaphore_signal(barrier, inc=1, device_id={"rows": peer(d)}, device_id_type=MESH)
-        return carry
-
-    lax.fori_loop(1, BLOCKS, greet, 0)
+    for slot in OTHERS:
+        pl.semaphore_signal(barrier, inc=1, device_id=peer(slot), device_id_type=MESH)
     for e in range(1, YS):
         pl.semaphore_signal(
             barrier, inc=1, device_id={"rep": (my_y + e) % YS}, device_id_type=MESH
         )
+
+    bring[0].wait()
+    cums[...] = jnp.zeros_like(cums)
+
+    places = iota((256, ROWS), 0).astype(f32).astype(bf16)
+
+    def count_link(k, carry):
+        row = nbt_ref[pl.ds(k, 1), :]
+        low_row = (row & 255).astype(f32).astype(bf16)
+        high_row = (row >> 8).astype(f32).astype(bf16)
+        low = narrow_hot(places == low_row)
+        high = narrow_hot(places == high_row)
+        cums[...] += dot(low, high, ((1,), (1,)))
+        return carry
+
+    lax.fori_loop(0, LINKS, count_link, 0)
+
+    def relative(high):
+        block = high >> 2
+        dx, dz, dc = ((block >> 4) - mx) & 3, ((block >> 1) - mz) & 7, (block - mc) & 1
+        turn = jnp.where(dz > 4, 2 * (dz - 4), jnp.maximum(2 * (4 - dz) - 1, 0))
+        return (turn << 3) | (dx << 1) | dc
+
+    high_row = iota((256, 256), 1)
+    rel_row = relative(high_row)
+    named = one_hot((cums[...] > 0.5) & (rel_row != OWN))
+    up_to = one_hot(iota((256, 256), 1) <= iota((256, 256), 0))
+    earlier = one_hot(
+        ((iota((256, 256), 0) >> 2) == (iota((256, 256), 1) >> 2))
+        & (iota((256, 256), 0) < iota((256, 256), 1))
+    )
+    before = dot(jnp.ones((256, 256), bf16), named).astype(bf16)
+    cums[...] = dot(up_to, named) + dot(before, earlier)
+    narrow = jnp.minimum(cums[...], 255.0).astype(bf16)
+    for s in range(SLOTS):
+        under = narrow_hot(narrow <= float(s))
+        while under.shape[0] > 16:
+            under = under[: under.shape[0] // 2] + under[under.shape[0] // 2 :]
+        counts[pl.ds(s, 1), :] = jnp.sum(under.astype(f32), axis=0, keepdims=True)
+    count = jnp.concatenate([counts[...].astype(bf16)] * 4, axis=0)
+    to_row = one_hot(iota((BLOCKS, 256), 0) == relative(iota((BLOCKS, 256), 1)))
+    asked = dot(to_row, count, ((1,), (1,)))
+    for slot in OTHERS:
+        req_out[slot] = asked[slot : slot + 1, :]
+
+    pl.semaphore_wait(barrier, BLOCKS - 1 + YS - 1)
+
+    for slot in OTHERS:
+        send(req_out.at[slot], req_in.at[mirrored(slot)], send_req, recv_req, peer(slot))
 
     wide = jnp.concatenate(
         [nbt_ref[...].astype(f32), jnp.zeros((128 - LINKS, ROWS), f32)], axis=0
@@ -91,66 +157,17 @@
                 turned[:, k : k + 1], (128, 128)
             )
 
-    cums[...] = jnp.zeros_like(cums)
-
-    def count_link(k, carry):
-        row = nbt_ref[pl.ds(k, 1), :]
-        total = jnp.zeros((256, 256), f32)
-        for quarter in range(4):
-            span = slice(quarter * 256, (quarter + 1) * 256)
-            low = one_hot(iota((256, 256), 0) == (row[:, span] & 255))
-            column = nbb[k, span, :] >> 8
-            high = jnp.concatenate(
-                [one_hot(iota((256, 128), 1) == column), one_hot(iota((256, 128), 1) + 128 == column)],
-                axis=1,
-            )
-            total = total + dot(low, high)
-        cums[...] += total
-        return carry
-
-    lax.fori_loop(0, LINKS, count_link, 0)
-
-    def relative(high):
-        block = high >> 2
-        x, z, c = block >> 4, (block >> 1) & 7, block & 1
-        return (((x - mx) & 3) << 4) | (((z - mz) & 7) << 1) | ((c - mc) & 1)
-
-    high_row = iota((256, 256), 1)
-    rel_row = relative(high_row)
-    named = one_hot((cums[...] > 0.5) & (rel_row != 0))
-    up_to = one_hot(iota((256, 256), 1) <= iota((256, 256), 0))
-    earlier = one_hot(
-        ((iota((256, 256), 0) >> 2) == (iota((256, 256), 1) >> 2))
-        & (iota((256, 256), 0) < iota((256, 256), 1))
-    )
-    before = dot(jnp.ones((256, 256), bf16), named).astype(bf16)
-    cums[...] = dot(up_to, named) + dot(before, earlier)
-    for s in range(SLOTS):
-        counts[pl.ds(s, 1), :] = jnp.sum(
-            jnp.where(cums[...] <= float(s), 1.0, 0.0), axis=0, keepdims=True
-        )
-    count = jnp.concatenate([counts[...].astype(bf16)] * 4, axis=0)
-    to_row = one_hot(iota((BLOCKS, 256), 0) == relative(iota((BLOCKS, 256), 1)))
-    asked = dot(to_row, count, ((1,), (1,)))
-    for d in range(BLOCKS):
-        req_out[d] = asked[d : d + 1, :]
-
-    pl.semaphore_wait(barrier, BLOCKS - 1 + YS - 1)
-
-    def ask(d, carry):
-        send(req_out.at[d], req_in.at[mirrored(d)], send_req, recv_req, {"rows": peer(d)})
-        return carry
-
-    lax.fori_loop(1, BLOCKS, ask, 0)
 
     quarter_of = (relative(iota((128, 256), 1)) & 3) == (iota((128, 256), 0) >> 5)
     four = jnp.where(quarter_of, count.astype(f32), 0.0).astype(bf16)
     chunks = BLOCKS * SLOTS // 128
     to_chunk = one_hot(iota((chunks, 256), 0) == (relative(iota((chunks, 256), 1)) >> 2))
     offset = dot(to_chunk, four, ((1,), (1,))).astype(i32)
-    rel = iota((chunks, 128), 0) * 4 + (iota((chunks, 128), 1) >> 5)
+    slots = iota((chunks, 128), 0) * 4 + (iota((chunks, 128), 1) >> 5)
+    turn = slots >> 3
+    dz = jnp.where(turn == 7, 0, jnp.where((turn & 1) == 0, 4 + (turn >> 1), 4 - ((turn + 1) >> 1)))
     owner = (
-        (((rel >> 4) + mx) & 3) * (ZS * CS) + ((((rel >> 1) & 7) + mz) & 7) * CS + ((rel + mc) & 1)
+        ((((slots >> 1) & 3) + mx) & 3) * (ZS * CS) + ((dz + mz) & 7) * CS + ((slots + mc) & 1)
     )
     far_ids = jnp.where(offset < ROWS, owner * ROWS + offset, -1)
     near_ids = me * ROWS + iota((ROWS // 128, 128), 0) * 128 + iota((ROWS // 128, 128), 1)
@@ -158,11 +175,13 @@
         cols[c] = jnp.broadcast_to(near_ids[c : c + 1, :], (8, 128))
     for c in range(chunks):
         cols[ROWS // 128 + c] = jnp.broadcast_to(far_ids[c : c + 1, :], (8, 128))
-    arrived[0] = jnp.zeros((SLOTS, COLS), bf16)
-
-    wait_for(req_in.at[pl.ds(1, BLOCKS - 1)], recv_req)
+    arrived[OWN] = jnp.zeros((SLOTS, COLS), bf16)
+    for copy in bring[1:]:
+        copy.wait()
+
+    wait_for(req_in.at[pl.ds(0, BLOCKS - 1)], recv_req)
     wanted = jnp.concatenate(
-        [req_in[d] if d else jnp.full((1, 128), float(ROWS), f32) for d in range(BLOCKS)]
+        [req_in[d] if d != OWN else jnp.full((1, 128), float(ROWS), f32) for d in range(BLOCKS)]
         + [jnp.zeros((128 - BLOCKS, 128), f32)],
         axis=0,
     )
@@ -175,12 +194,11 @@
         taken = dot(pick[...], gal_ref[...]).astype(bf16)
         for j in range(GROUP):
             picked[group * GROUP + j] = taken[j * SLOTS : (j + 1) * SLOTS, :]
-        for j in range(GROUP):
-            d = group * GROUP + j
-            if d:
+        for slot in range(group * GROUP, (group + 1) * GROUP):
+            if slot != OWN:
                 send(
-                    picked.at[d], arrived.at[mirrored(d)], send_rep,
-                    recv_rep.at[mirrored(d) // GROUP], {"rows": peer(d)},
+                    picked.at[slot], arrived.at[mirrored(slot)], send_rep,
+                    recv_rep.at[mirrored(slot) // GROUP], peer(slot),
                 )
 
     def choose(block, carry):
@@ -209,11 +227,10 @@
     query_sq = jnp.sum(q_t * q_t, axis=0, keepdims=True)
 
     for group in range(GROUPS):
-        first_slot = 1 if group == 0 else group * GROUP
-        last_slot = (group + 1) * GROUP
-        wait_for(arrived.at[pl.ds(first_slot, last_slot - first_slot)], recv_rep.at[group])
+        coming = GROUP - (OWN // GROUP == group)
+        wait_for(arrived.at[pl.ds(group * GROUP, coming)], recv_rep.at[group])
         begin = ROWS + group * GROUP * SLOTS
-        rows = arrived[group * GROUP : last_slot].reshape(GROUP * SLOTS, COLS)
+        rows = arrived[group * GROUP : (group + 1) * GROUP].reshape(GROUP * SLOTS, COLS)
         acc[...] += dot(sel[:, begin : begin + GROUP * SLOTS], rows)
 
     augmented = (acc[...] * (1.0 / (2 * LINKS))).astype(bf16)
@@ -261,7 +278,7 @@
 
     def two_rows(total):
         high = total.astype(bf16).astype(f32)
-        at = iota((16, QUERIES), 0)
+        at = iota((TAIL, QUERIES), 0)
         return jnp.where(at == 0, high, jnp.where(at == 1, total - high, 0.0)).astype(bf16)
 
     slice_rows = COLS // (XS * CS)
@@ -340,8 +357,8 @@
         total = total + fp_in[e].astype(f32)
     final_ref[...] = total * e_mine * row_scale
 
-    wait_for(req_out.at[pl.ds(1, BLOCKS - 1)], send_req)
-    wait_for(picked.at[pl.ds(1, BLOCKS - 1)], send_rep)
+    wait_for(req_out.at[pl.ds(0, BLOCKS - 1)], send_req)
+    wait_for(picked.at[pl.ds(0, BLOCKS - 1)], send_rep)
     wait_for(lsq_in.at[pl.ds(1, YS - 1)], send_y.at[0])
     wait_for(rsq_in.at[pl.ds(1, YS - 1)], send_y.at[1])
     wait_for(ft_in.at[pl.ds(1, YS - 1)], send_y.at[2])
@@ -352,21 +369,35 @@
     wait_for(fp_in.at[pl.ds(1, YS - 1)], send_e.at[1])
 
 
+def hand_over(aug_in, first_in, final_in, aug_out, first_out, final_out, sems):
+    pairs = ((aug_in, aug_out), (first_in, first_out), (final_in, final_out))
+    copies = [pltpu.make_async_copy(a, b, sems.at[i]) for i, (a, b) in enumerate(pairs)]
+    for copy in copies:
+        copy.start()
+    for copy in copies:
+        copy.wait()
+
+
 def local(gallery, neighbours, queries, listed):
     vmem = pl.BlockSpec(memory_space=pltpu.VMEM)
     slice_rows = COLS // (XS * CS)
     columns = ROWS + BLOCKS * SLOTS
     dma = pltpu.SemaphoreType.DMA
-    return pl.pallas_call(
+    results = (
+        jax.ShapeDtypeStruct((ROWS, COLS), bf16),
+        jax.ShapeDtypeStruct((SHARE, ROWS), f32),
+        jax.ShapeDtypeStruct((SHARE, ROWS), f32),
+    )
+    made = pl.pallas_call(
         kernel,
-        out_shape=(
-            jax.ShapeDtypeStruct((ROWS, COLS), bf16),
-            jax.ShapeDtypeStruct((SHARE, ROWS), f32),
-            jax.ShapeDtypeStruct((SHARE, ROWS), f32),
-        ),
-        in_specs=[vmem] * 4,
+        out_shape=tuple(pltpu.VMEM(r.shape, r.dtype) for r in results),
+        in_specs=[pl.BlockSpec(memory_space=pltpu.HBM)] * 4,
         out_specs=(vmem,) * 3,
         scratch_shapes=[
+            pltpu.VMEM((ROWS, COLS), bf16),
+            pltpu.VMEM((LINKS, ROWS), i32),
+            pltpu.VMEM((QUERIES, COLS), bf16),
+            pltpu.VMEM((LINKS, QUERIES), i32),
             pltpu.VMEM((LINKS, ROWS, 128), i32),
             pltpu.VMEM((256, 256), f32),
             pltpu.VMEM((SLOTS, 256), f32),
@@ -387,10 +418,10 @@
             pltpu.VMEM((YS, SHARE, ROWS), bf16),
             pltpu.VMEM((1, ROWS), f32),
             pltpu.VMEM((YS, 1, ROWS), f32),
-            pltpu.VMEM((XS * CS, slice_rows + 16, QUERIES), bf16),
-            pltpu.VMEM((XS * CS, slice_rows + 16, QUERIES), bf16),
-            pltpu.VMEM((slice_rows + 16, QUERIES), bf16),
-            pltpu.VMEM((ZS, slice_rows + 16, QUERIES), bf16),
+            pltpu.VMEM((XS * CS, slice_rows + TAIL, QUERIES), bf16),
+            pltpu.VMEM((XS * CS, slice_rows + TAIL, QUERIES), bf16),
+            pltpu.VMEM((slice_rows + TAIL, QUERIES), bf16),
+            pltpu.VMEM((ZS, slice_rows + TAIL, QUERIES), bf16),
             pltpu.VMEM((slice_rows, QUERIES), bf16),
             pltpu.VMEM((XS * CS, slice_rows, QUERIES), bf16),
             pltpu.VMEM((1, QUERIES), f32),
@@ -398,13 +429,22 @@
             pltpu.VMEM((YS, SHARE, ROWS), bf16),
             pltpu.VMEM((YS, SHARE, ROWS), bf16),
             pltpu.VMEM((QUERIES, QUERIES), f32),
-            dma, dma, dma, dma((GROUPS,)), dma((3,)), dma((3,)), dma((3,)), dma((3,)), dma((2,)), dma((2,)),
+            dma((4,)), dma, dma, dma, dma((GROUPS,)), dma((3,)), dma((3,)), dma((3,)), dma((3,)), dma((2,)), dma((2,)),
         ],
         compiler_params=pltpu.CompilerParams(
-            collective_id=0, has_side_effects=True, vmem_limit_bytes=60 * 1024 * 1024
+            collective_id=0, has_side_effects=True, vmem_limit_bytes=66100000
         ),
         name="expand",
     )(gallery, neighbours.T, queries, listed.T)
+    return pl.pallas_call(
+        hand_over,
+        out_shape=results,
+        in_specs=[vmem] * 3,
+        out_specs=(pl.BlockSpec(memory_space=pl.ANY),) * 3,
+        scratch_shapes=[dma((3,))],
+        compiler_params=pltpu.CompilerParams(vmem_limit_bytes=4 * 1024 * 1024),
+        name="hand_over",
+    )(*made)
 
 
 def solution(mesh):

time: 79.7 us -> 69.7 us (0.87)
  Pallas kernels: 75.4 us -> 69 us
  local copies, waits for them, and re-layouts: 3.51 us -> 0 us
    pallas_call x1 -> x2, Pallas kernels: 75.4 us -> 69 us  [the longest x1 68.1 us: local(): pl.pallas_call(kernel, out_shape=tuple((pltpu.VMEM(r.shape, r.dtype) for...]
    unnamed x7 -> x0, local copies, waits for them, and re-layouts: 3.51 us -> none
where the time goes in v2:
time: 69.7 us; the launch traced here: 69.6 us
  Pallas kernels  69 us (99%)
    pallas_call x1, Pallas kernels, local(): pl.pallas_call(kernel, out_shape=tuple((pltpu.VMEM(r.shape, r.dtype) for...  68.1 us

profile of v2, /device:TPU:1, one launch (start us, length us, event | category | flops | bytes accessed | tf_op | source)
XLA Modules:
  0.0 69.6 jit_solution(9481623656785917466)
XLA Ops:
  0.6 68.1 %expand.1 = (bf16[1024,256]{1,0:T(8,128)(2,1)S(1)}, f32[32,1024]{1,0:T(8,128)S(1)}, f32[32,1024]{1,0:T(8,128)S(1)}) custom-call(bf16[1024,256]{1,0:T(8,128)(2,1)} %gal_far.1, s32[10,1024]{1,0:T(8,128)} %bitcast.2, bf16[128,256]{1,0:T(8,128)(2,1)} %q_far.1, s32[10,128]{1,0:T(8,128)} %bitcast.3), custom_call_target="tpu_custom_call" | custom-call | tf_op jit(solution)/shard_map/expand/pallas_call | solution.py:391
  68.7 0.9 %hand_over.1 = (bf16[1024,256]{1,0:T(8,128)(2,1)}, f32[32,1024]{1,0:T(8,128)}, f32[32,1024]{1,0:T(8,128)}) custom-call(bf16[1024,256]{1,0:T(8,128)(2,1)S(1)} %get-tuple-element.6.aug_in, f32[32,1024]{1,0:T(8,128)S(1)} %get-tuple-element.7.first_in, f32[32,1024]{1,0:T(8,128)S(1)} %get-tuple-element.8.final_in), custom_call_target="tpu_custom_call" | custom-call | tf_op jit(solution)/shard_map/hand_over/pallas_call | solution.py:439

commit v3 on v2

--- a/solution.py
+++ b/solution.py
@@ -23,20 +23,26 @@
 TAIL = 8
 
 
-FAR_FIRST = (4, 3, 5, 2, 6, 1, 7, 0)
+STEPS = (1, 7, 4, 3, 5, 2, 6, 0)
 OWN = (ZS - 1) * XS * CS
 
 
 def split_offset(slot):
-    return (slot // CS) % XS, FAR_FIRST[slot // (XS * CS)], slot % CS
+    return (slot // CS) % XS, STEPS[slot // (XS * CS)], slot % CS
 
 
 def mirrored(slot):
     dx, dz, dc = split_offset(slot)
-    return FAR_FIRST.index((ZS - dz) % ZS) * (XS * CS) + ((XS - dx) % XS) * CS + dc
+    return STEPS.index((ZS - dz) % ZS) * (XS * CS) + ((XS - dx) % XS) * CS + dc
+
+
+def hops(slot):
+    dx, dz, dc = split_offset(slot)
+    return min(dx, XS - dx) + min(dz, ZS - dz)
 
 
 OTHERS = tuple(slot for slot in range(BLOCKS) if slot != OWN)
+FARTHEST = tuple(sorted(OTHERS, key=hops, reverse=True))
 
 
 def iota(shape, dim):
@@ -91,7 +97,7 @@
         copy.start()
     barrier = pltpu.get_barrier_semaphore()
 
-    for slot in OTHERS:
+    for slot in FARTHEST:
         pl.semaphore_signal(barrier, inc=1, device_id=peer(slot), device_id_type=MESH)
     for e in range(1, YS):
         pl.semaphore_signal(
@@ -99,30 +105,26 @@
         )
 
     bring[0].wait()
-    cums[...] = jnp.zeros_like(cums)
-
     places = iota((256, ROWS), 0).astype(f32).astype(bf16)
-
-    def count_link(k, carry):
-        row = nbt_ref[pl.ds(k, 1), :]
-        low_row = (row & 255).astype(f32).astype(bf16)
-        high_row = (row >> 8).astype(f32).astype(bf16)
-        low = narrow_hot(places == low_row)
-        high = narrow_hot(places == high_row)
-        cums[...] += dot(low, high, ((1,), (1,)))
-        return carry
-
-    lax.fori_loop(0, LINKS, count_link, 0)
+    named = None
+    for k in range(LINKS):
+        row = nbt_ref[k : k + 1, :]
+        low, high = [
+            narrow_hot(places == part.astype(f32).astype(bf16)).astype(jnp.float8_e4m3fn)
+            for part in (row & 255, row >> 8)
+        ]
+        found = dot(low, high, ((1,), (1,)))
+        named = found if named is None else named + found
 
     def relative(high):
         block = high >> 2
         dx, dz, dc = ((block >> 4) - mx) & 3, ((block >> 1) - mz) & 7, (block - mc) & 1
-        turn = jnp.where(dz > 4, 2 * (dz - 4), jnp.maximum(2 * (4 - dz) - 1, 0))
+        turn = sum(jnp.where(dz == step, at, 0) for at, step in enumerate(STEPS) if at)
         return (turn << 3) | (dx << 1) | dc
 
     high_row = iota((256, 256), 1)
     rel_row = relative(high_row)
-    named = one_hot((cums[...] > 0.5) & (rel_row != OWN))
+    named = one_hot((named > 0.5) & (rel_row != OWN))
     up_to = one_hot(iota((256, 256), 1) <= iota((256, 256), 0))
     earlier = one_hot(
         ((iota((256, 256), 0) >> 2) == (iota((256, 256), 1) >> 2))
@@ -144,8 +146,9 @@
 
     pl.semaphore_wait(barrier, BLOCKS - 1 + YS - 1)
 
-    for slot in OTHERS:
-        send(req_out.at[slot], req_in.at[mirrored(slot)], send_req, recv_req, peer(slot))
+    for slot in FARTHEST:
+        there = mirrored(slot)
+        send(req_out.at[slot], req_in.at[there], send_req, recv_req.at[there // GROUP], peer(slot))
 
     wide = jnp.concatenate(
         [nbt_ref[...].astype(f32), jnp.zeros((128 - LINKS, ROWS), f32)], axis=0
@@ -164,8 +167,7 @@
     to_chunk = one_hot(iota((chunks, 256), 0) == (relative(iota((chunks, 256), 1)) >> 2))
     offset = dot(to_chunk, four, ((1,), (1,))).astype(i32)
     slots = iota((chunks, 128), 0) * 4 + (iota((chunks, 128), 1) >> 5)
-    turn = slots >> 3
-    dz = jnp.where(turn == 7, 0, jnp.where((turn & 1) == 0, 4 + (turn >> 1), 4 - ((turn + 1) >> 1)))
+    dz = sum(jnp.where((slots >> 3) == at, step, 0) for at, step in enumerate(STEPS))
     owner = (
         ((((slots >> 1) & 3) + mx) & 3) * (ZS * CS) + ((dz + mz) & 7) * CS + ((slots + mc) & 1)
     )
@@ -179,17 +181,16 @@
     for copy in bring[1:]:
         copy.wait()
 
-    wait_for(req_in.at[pl.ds(0, BLOCKS - 1)], recv_req)
-    wanted = jnp.concatenate(
-        [req_in[d] if d != OWN else jnp.full((1, 128), float(ROWS), f32) for d in range(BLOCKS)]
-        + [jnp.zeros((128 - BLOCKS, 128), f32)],
-        axis=0,
-    )
-    wanted = jnp.transpose(wanted).astype(i32)
     for group in range(GROUPS):
+        coming = GROUP - (OWN // GROUP == group)
+        wait_for(req_in.at[pl.ds(group * GROUP, coming)], recv_req.at[group])
+        wanted = [
+            jnp.full((1, 128), float(ROWS), f32) if slot == OWN else req_in[slot]
+            for slot in range(group * GROUP, (group + 1) * GROUP)
+        ]
+        wanted = jnp.transpose(jnp.concatenate(wanted, axis=0)).astype(i32)
         for j in range(GROUP):
-            d = group * GROUP + j
-            place = wanted[0:SLOTS, d : d + 1]
+            place = wanted[0:SLOTS, j : j + 1]
             pick[j * SLOTS : (j + 1) * SLOTS, :] = one_hot(iota((SLOTS, ROWS), 1) == place)
         taken = dot(pick[...], gal_ref[...]).astype(bf16)
         for j in range(GROUP):
@@ -255,15 +256,6 @@
     for e in (2, 1, 3):
         send(lsq_out, lsq_in.at[YS - e], send_y.at[0], recv_y.at[0], y_peer(e))
 
-    row_sq = jnp.sum(aug_t * aug_t, axis=0, keepdims=True)
-    rsq_out[...] = row_sq
-    first = dot(q_ref[...], augt[...])
-    for y in range(YS):
-        ft_out[y] = first[y * SHARE : (y + 1) * SHARE, :].astype(bf16)
-    for e in (2, 1, 3):
-        send(rsq_out, rsq_in.at[YS - e], send_y.at[1], recv_y.at[1], y_peer(e))
-        send(ft_out.at[(my_y + e) % YS], ft_in.at[YS - e], send_y.at[2], recv_y.at[2], y_peer(e))
-
     wait_for(lsq_in.at[pl.ds(1, YS - 1)], recv_y.at[0])
     sums = lsq_out[...] + lsq_in[1] + lsq_in[2] + lsq_in[3]
     q_scale = lax.rsqrt(sums[2 * LINKS : 2 * LINKS + 1, :] + epsilon)
@@ -299,6 +291,15 @@
             part.at[px * CS + pc], part_in.at[back], send_p.at[0], recv_p.at[0],
             {"rows": px * (ZS * CS) + mz * CS + pc},
         )
+    wide_t = augt[...].astype(f32)
+    rsq_out[...] = jnp.sum(wide_t * wide_t, axis=0, keepdims=True)
+    first = dot(q_ref[...], augt[...])
+    for y in range(YS):
+        ft_out[y] = first[y * SHARE : (y + 1) * SHARE, :].astype(bf16)
+    for e in (2, 1, 3):
+        send(rsq_out, rsq_in.at[YS - e], send_y.at[1], recv_y.at[1], y_peer(e))
+        send(ft_out.at[(my_y + e) % YS], ft_in.at[YS - e], send_y.at[2], recv_y.at[2], y_peer(e))
+
     wait_for(part_in.at[pl.ds(1, XS * CS - 1)], recv_p.at[0])
     so_far = part[mine].astype(f32)
     for e in range(1, XS * CS):
@@ -310,18 +311,6 @@
             half, half_in.at[ZS - e], send_p.at[1], recv_p.at[1],
             {"rows": mx * (ZS * CS) + ((mz + e) % ZS) * CS + mc},
         )
-
-    wait_for(rsq_in.at[pl.ds(1, YS - 1)], recv_y.at[1])
-    wait_for(ft_in.at[pl.ds(1, YS - 1)], recv_y.at[2])
-    row_scale = lax.rsqrt(rsq_out[...] + rsq_in[1] + rsq_in[2] + rsq_in[3] + epsilon)
-    q_col = jnp.transpose(jnp.broadcast_to(q_scale * logit_scale, (QUERIES, QUERIES)))
-    esq_col[...] = q_col
-    mine_q = pl.ds(pl.multiple_of(my_y * SHARE, SHARE), SHARE)
-    q_mine = esq_col[mine_q, 0:1]
-    total = ft_out[my_y].astype(f32)
-    for e in range(1, YS):
-        total = total + ft_in[e].astype(f32)
-    first_ref[...] = total * q_mine * row_scale
 
     wait_for(half_in.at[pl.ds(1, ZS - 1)], recv_p.at[1])
     so_far = half[...].astype(f32)
@@ -335,6 +324,18 @@
             piece, whole.at[mine], send_p.at[2], recv_p.at[2],
             {"rows": px * (ZS * CS) + mz * CS + pc},
         )
+    wait_for(rsq_in.at[pl.ds(1, YS - 1)], recv_y.at[1])
+    wait_for(ft_in.at[pl.ds(1, YS - 1)], recv_y.at[2])
+    row_scale = lax.rsqrt(rsq_out[...] + rsq_in[1] + rsq_in[2] + rsq_in[3] + epsilon)
+    q_col = jnp.transpose(jnp.broadcast_to(q_scale * logit_scale, (QUERIES, QUERIES)))
+    esq_col[...] = q_col
+    mine_q = pl.ds(pl.multiple_of(my_y * SHARE, SHARE), SHARE)
+    q_mine = esq_col[mine_q, 0:1]
+    total = ft_out[my_y].astype(f32)
+    for e in range(1, YS):
+        total = total + ft_in[e].astype(f32)
+    first_ref[...] = total * q_mine * row_scale
+
     wait_for(whole.at[pl.ds(1, XS * CS - 1)], recv_p.at[2])
     whole[mine] = piece[...]
 
@@ -429,7 +430,7 @@
             pltpu.VMEM((YS, SHARE, ROWS), bf16),
             pltpu.VMEM((YS, SHARE, ROWS), bf16),
             pltpu.VMEM((QUERIES, QUERIES), f32),
-            dma((4,)), dma, dma, dma, dma((GROUPS,)), dma((3,)), dma((3,)), dma((3,)), dma((3,)), dma((2,)), dma((2,)),
+            dma((4,)), dma, dma((GROUPS,)), dma, dma((GROUPS,)), dma((3,)), dma((3,)), dma((3,)), dma((3,)), dma((2,)), dma((2,)),
         ],
         compiler_params=pltpu.CompilerParams(
             collective_id=0, has_side_effects=True, vmem_limit_bytes=66100000

time: 69.7 us -> 67.7 us (0.971)
  Pallas kernels: 69 us -> 66.8 us
    pallas_call x1, Pallas kernels: 68.1 us -> 65.9 us  [local(): pl.pallas_call(kernel, out_shape=tuple((pltpu.VMEM(r.shape, r.dtype) for...]
where the time goes in v3:
time: 67.7 us; the launch traced here: 67.6 us
  Pallas kernels  66.8 us (99%)
  between operations  0.8 us (1%)
    pallas_call x1, Pallas kernels, local(): pl.pallas_call(kernel, out_shape=tuple((pltpu.VMEM(r.shape, r.dtype) for...  65.9 us

profile of v3, /device:TPU:1, one launch (start us, length us, event | category | flops | bytes accessed | tf_op | source)
XLA Modules:
  0.0 67.6 jit_solution(12022166416565619191)
XLA Ops:
  0.6 65.9 %expand.1 = (bf16[1024,256]{1,0:T(8,128)(2,1)S(1)}, f32[32,1024]{1,0:T(8,128)S(1)}, f32[32,1024]{1,0:T(8,128)S(1)}) custom-call(bf16[1024,256]{1,0:T(8,128)(2,1)} %gal_far.1, s32[10,1024]{1,0:T(8,128)} %bitcast.2, bf16[128,256]{1,0:T(8,128)(2,1)} %q_far.1, s32[10,128]{1,0:T(8,128)} %bitcast.3), custom_call_target="tpu_custom_call" | custom-call | tf_op jit(solution)/shard_map/expand/pallas_call | solution.py:392
  66.6 0.9 %hand_over.1 = (bf16[1024,256]{1,0:T(8,128)(2,1)}, f32[32,1024]{1,0:T(8,128)}, f32[32,1024]{1,0:T(8,128)}) custom-call(bf16[1024,256]{1,0:T(8,128)(2,1)S(1)} %get-tuple-element.6.aug_in, f32[32,1024]{1,0:T(8,128)S(1)} %get-tuple-element.7.first_in, f32[32,1024]{1,0:T(8,128)S(1)} %get-tuple-element.8.final_in), custom_call_target="tpu_custom_call" | custom-call | tf_op jit(solution)/shard_map/hand_over/pallas_call | solution.py:440

commit v4 on v3

--- a/solution.py
+++ b/solution.py
@@ -20,7 +20,6 @@
 SHARE = QUERIES // YS
 GROUP = 8
 GROUPS = BLOCKS // GROUP
-TAIL = 8
 
 
 STEPS = (1, 7, 4, 3, 5, 2, 6, 0)
@@ -70,8 +69,8 @@
     aug_ref, first_ref, final_ref,
     gal_ref, nbt_ref, q_ref, lst_ref, nbb, cums, counts, req_out, req_in, cols, sel, picked, arrived, pick, acc, augt, rows_t, lsb,
     lsq_out, lsq_in, ft_out, ft_in, rsq_out, rsq_in,
-    part, part_in, half, half_in, piece, whole, esq_out, esq_in, fp_out, fp_in, esq_col,
-    sem_in, send_req, recv_req, send_rep, recv_rep, send_y, recv_y, send_p, recv_p, send_e, recv_e,
+    part, part_in, half, half_in, piece, whole, den_out, den_in, den_far, esq_out, esq_in, fp_out, fp_in, esq_col,
+    sem_in, send_req, recv_req, send_rep, recv_rep, send_y, recv_y, send_p, recv_p, send_e, recv_e, send_d, recv_d,
 ):
     me = lax.axis_index("rows")
     my_y = lax.axis_index("rep")
@@ -215,8 +214,9 @@
         return carry
 
     lax.fori_loop(0, ROWS // 16, choose, 0)
-    acc[...] = float(2 * LINKS) * gal_ref[...].astype(f32)
-    acc[...] += dot(sel[:, :ROWS], gal_ref[...])
+    gal_t = jnp.transpose(gal_ref[...].astype(f32))
+    acc[...] = float(2 * LINKS) * gal_t
+    acc[...] += dot(gal_t.astype(bf16), sel[:, :ROWS], ((1,), (1,)))
 
     owned = lst_ref[...] >> 10
     inside = jnp.where(owned == me, lst_ref[...] & (ROWS - 1), -1)
@@ -232,12 +232,10 @@
         wait_for(arrived.at[pl.ds(group * GROUP, coming)], recv_rep.at[group])
         begin = ROWS + group * GROUP * SLOTS
         rows = arrived[group * GROUP : (group + 1) * GROUP].reshape(GROUP * SLOTS, COLS)
-        acc[...] += dot(sel[:, begin : begin + GROUP * SLOTS], rows)
-
-    augmented = (acc[...] * (1.0 / (2 * LINKS))).astype(bf16)
-    aug_ref[...] = augmented
-    aug_t = jnp.transpose(augmented.astype(f32))
-    augt[...] = aug_t.astype(bf16)
+        rows = jnp.transpose(rows.astype(f32)).astype(bf16)
+        acc[...] += dot(rows, sel[:, begin : begin + GROUP * SLOTS], ((1,), (1,)))
+
+    augt[...] = (acc[...] * (1.0 / (2 * LINKS))).astype(bf16)
 
     def y_peer(e):
         return {"rep": (my_y + e) % YS}
@@ -256,6 +254,8 @@
     for e in (2, 1, 3):
         send(lsq_out, lsq_in.at[YS - e], send_y.at[0], recv_y.at[0], y_peer(e))
 
+    aug_ref[...] = jnp.transpose(augt[...].astype(f32)).astype(bf16)
+
     wait_for(lsq_in.at[pl.ds(1, YS - 1)], recv_y.at[0])
     sums = lsq_out[...] + lsq_in[1] + lsq_in[2] + lsq_in[3]
     q_scale = lax.rsqrt(sums[2 * LINKS : 2 * LINKS + 1, :] + epsilon)
@@ -268,16 +268,10 @@
         denom = denom + weight
         numer = numer + rows_t[:, k * 128 : (k + 1) * 128] * (weight * unit)
 
-    def two_rows(total):
-        high = total.astype(bf16).astype(f32)
-        at = iota((TAIL, QUERIES), 0)
-        return jnp.where(at == 0, high, jnp.where(at == 1, total - high, 0.0)).astype(bf16)
-
     slice_rows = COLS // (XS * CS)
-    tail = two_rows(denom)
+    den_out[0] = denom
     for i in range(XS * CS):
-        part[i, 0:slice_rows] = numer[i * slice_rows : (i + 1) * slice_rows, :].astype(bf16)
-        part[i, slice_rows:] = tail
+        part[i] = numer[i * slice_rows : (i + 1) * slice_rows, :].astype(bf16)
     mine = mx * CS + mc
 
     def near(e):
@@ -287,6 +281,10 @@
     order = (4, 5, 2, 3, 6, 7, 1)
     for e in order:
         px, pc, back = near(e)
+        send(
+            den_out.at[0], den_in.at[back], send_d.at[0], recv_d.at[0],
+            {"rows": px * (ZS * CS) + mz * CS + pc},
+        )
         send(
             part.at[px * CS + pc], part_in.at[back], send_p.at[0], recv_p.at[0],
             {"rows": px * (ZS * CS) + mz * CS + pc},
@@ -304,9 +302,14 @@
     so_far = part[mine].astype(f32)
     for e in range(1, XS * CS):
         so_far = so_far + part_in[e].astype(f32)
-    half[0:slice_rows] = so_far[0:slice_rows].astype(bf16)
-    half[slice_rows:] = two_rows(so_far[slice_rows : slice_rows + 1] + so_far[slice_rows + 1 : slice_rows + 2])
+    half[...] = so_far.astype(bf16)
+    wait_for(den_in.at[pl.ds(1, XS * CS - 1)], recv_d.at[0])
+    den_out[1] = sum((den_in[e] for e in range(1, XS * CS)), den_out[0])
     for e in (4, 3, 5, 2, 6, 1, 7):
+        send(
+            den_out.at[1], den_far.at[ZS - e], send_d.at[1], recv_d.at[1],
+            {"rows": mx * (ZS * CS) + ((mz + e) % ZS) * CS + mc},
+        )
         send(
             half, half_in.at[ZS - e], send_p.at[1], recv_p.at[1],
             {"rows": mx * (ZS * CS) + ((mz + e) % ZS) * CS + mc},
@@ -316,8 +319,9 @@
     so_far = half[...].astype(f32)
     for e in range(1, ZS):
         so_far = so_far + half_in[e].astype(f32)
-    denom = so_far[slice_rows : slice_rows + 1] + so_far[slice_rows + 1 : slice_rows + 2]
-    piece[...] = (so_far[0:slice_rows] / denom).astype(bf16)
+    wait_for(den_far.at[pl.ds(1, ZS - 1)], recv_d.at[1])
+    denom = sum((den_far[e] for e in range(1, ZS)), den_out[1])
+    piece[...] = (so_far / denom).astype(bf16)
     for e in order:
         px, pc, back = near(e)
         send(
@@ -366,6 +370,8 @@
     wait_for(part_in.at[pl.ds(1, XS * CS - 1)], send_p.at[0])
     wait_for(half_in.at[pl.ds(1, ZS - 1)], send_p.at[1])
     wait_for(whole.at[pl.ds(1, XS * CS - 1)], send_p.at[2])
+    wait_for(den_in.at[pl.ds(1, XS * CS - 1)], send_d.at[0])
+    wait_for(den_far.at[pl.ds(1, ZS - 1)], send_d.at[1])
     wait_for(esq_in.at[pl.ds(1, YS - 1)], send_e.at[0])
     wait_for(fp_in.at[pl.ds(1, YS - 1)], send_e.at[1])
 
@@ -409,7 +415,7 @@
             pltpu.VMEM((BLOCKS, SLOTS, COLS), bf16),
             pltpu.VMEM((BLOCKS, SLOTS, COLS), bf16),
             pltpu.VMEM((GROUP * SLOTS, ROWS), bf16),
-            pltpu.VMEM((ROWS, COLS), f32),
+            pltpu.VMEM((COLS, ROWS), f32),
             pltpu.VMEM((COLS, ROWS), bf16),
             pltpu.VMEM((COLS, LINKS * QUERIES), f32),
             pltpu.VMEM((ROWS, LINKS * QUERIES), bf16),
@@ -419,18 +425,21 @@
             pltpu.VMEM((YS, SHARE, ROWS), bf16),
             pltpu.VMEM((1, ROWS), f32),
             pltpu.VMEM((YS, 1, ROWS), f32),
-            pltpu.VMEM((XS * CS, slice_rows + TAIL, QUERIES), bf16),
-            pltpu.VMEM((XS * CS, slice_rows + TAIL, QUERIES), bf16),
-            pltpu.VMEM((slice_rows + TAIL, QUERIES), bf16),
-            pltpu.VMEM((ZS, slice_rows + TAIL, QUERIES), bf16),
+            pltpu.VMEM((XS * CS, slice_rows, QUERIES), bf16),
+            pltpu.VMEM((XS * CS, slice_rows, QUERIES), bf16),
+            pltpu.VMEM((slice_rows, QUERIES), bf16),
+            pltpu.VMEM((ZS, slice_rows, QUERIES), bf16),
             pltpu.VMEM((slice_rows, QUERIES), bf16),
             pltpu.VMEM((XS * CS, slice_rows, QUERIES), bf16),
+            pltpu.VMEM((2, 1, QUERIES), f32),
+            pltpu.VMEM((XS * CS, 1, QUERIES), f32),
+            pltpu.VMEM((ZS, 1, QUERIES), f32),
             pltpu.VMEM((1, QUERIES), f32),
             pltpu.VMEM((YS, 1, QUERIES), f32),
             pltpu.VMEM((YS, SHARE, ROWS), bf16),
             pltpu.VMEM((YS, SHARE, ROWS), bf16),
             pltpu.VMEM((QUERIES, QUERIES), f32),
-            dma((4,)), dma, dma((GROUPS,)), dma, dma((GROUPS,)), dma((3,)), dma((3,)), dma((3,)), dma((3,)), dma((2,)), dma((2,)),
+            dma((4,)), dma, dma((GROUPS,)), dma, dma((GROUPS,)), dma((3,)), dma((3,)), dma((3,)), dma((3,)), dma((2,)), dma((2,)), dma((2,)), dma((2,)),
         ],
         compiler_params=pltpu.CompilerParams(
             collective_id=0, has_side_effects=True, vmem_limit_bytes=66100000

time: 67.7 us -> 66.8 us (0.987)
  Pallas kernels: 66.8 us -> 65.9 us
    pallas_call x1, Pallas kernels: 65.9 us -> 65 us  [local(): pl.pallas_call(kernel, out_shape=tuple((pltpu.VMEM(r.shape, r.dtype) for...]
where the time goes in v4:
time: 66.8 us; the launch traced here: 66.7 us
  Pallas kernels  65.9 us (99%)
  between operations  0.8 us (1%)
    pallas_call x1, Pallas kernels, local(): pl.pallas_call(kernel, out_shape=tuple((pltpu.VMEM(r.shape, r.dtype) for...  65 us

profile of v4, /device:TPU:1, one launch (start us, length us, event | category | flops | bytes accessed | tf_op | source)
XLA Modules:
  0.0 66.7 jit_solution(13131906204236091118)
XLA Ops:
  0.6 65.0 %expand.1 = (bf16[1024,256]{1,0:T(8,128)(2,1)S(1)}, f32[32,1024]{1,0:T(8,128)S(1)}, f32[32,1024]{1,0:T(8,128)S(1)}) custom-call(bf16[1024,256]{1,0:T(8,128)(2,1)} %gal_far.1, s32[10,1024]{1,0:T(8,128)} %bitcast.2, bf16[128,256]{1,0:T(8,128)(2,1)} %q_far.1, s32[10,128]{1,0:T(8,128)} %bitcast.3), custom_call_target="tpu_custom_call" | custom-call | tf_op jit(solution)/shard_map/expand/pallas_call | solution.py:398
  65.6 0.9 %hand_over.1 = (bf16[1024,256]{1,0:T(8,128)(2,1)}, f32[32,1024]{1,0:T(8,128)}, f32[32,1024]{1,0:T(8,128)}) custom-call(bf16[1024,256]{1,0:T(8,128)(2,1)S(1)} %get-tuple-element.6.aug_in, f32[32,1024]{1,0:T(8,128)S(1)} %get-tuple-element.7.first_in, f32[32,1024]{1,0:T(8,128)S(1)} %get-tuple-element.8.final_in), custom_call_target="tpu_custom_call" | custom-call | tf_op jit(solution)/shard_map/hand_over/pallas_call | solution.py:449

commit v5 on v4

--- a/solution.py
+++ b/solution.py
@@ -136,8 +136,12 @@
         under = narrow_hot(narrow <= float(s))
         while under.shape[0] > 16:
             under = under[: under.shape[0] // 2] + under[under.shape[0] // 2 :]
-        counts[pl.ds(s, 1), :] = jnp.sum(under.astype(f32), axis=0, keepdims=True)
-    count = jnp.concatenate([counts[...].astype(bf16)] * 4, axis=0)
+        counts[s * 16 : (s + 1) * 16, :] = under
+    gather = narrow_hot(
+        (iota((SLOTS, SLOTS * 16), 1) >> 4).astype(f32).astype(bf16)
+        == iota((SLOTS, SLOTS * 16), 0).astype(f32).astype(bf16)
+    )
+    count = jnp.concatenate([dot(gather, counts[...]).astype(bf16)] * 4, axis=0)
     to_row = one_hot(iota((BLOCKS, 256), 0) == relative(iota((BLOCKS, 256), 1)))
     asked = dot(to_row, count, ((1,), (1,)))
     for slot in OTHERS:
@@ -407,7 +411,7 @@
             pltpu.VMEM((LINKS, QUERIES), i32),
             pltpu.VMEM((LINKS, ROWS, 128), i32),
             pltpu.VMEM((256, 256), f32),
-            pltpu.VMEM((SLOTS, 256), f32),
+            pltpu.VMEM((SLOTS * 16, 256), bf16),
             pltpu.VMEM((BLOCKS, 1, 128), f32),
             pltpu.VMEM((BLOCKS, 1, 128), f32),
             pltpu.VMEM((columns // 128, 8, 128), i32),

time: 66.8 us -> 66.8 us (level)
  no operation moved by 1% of the time
where the time goes in v5:
time: 66.8 us; the launch traced here: 66.7 us
  Pallas kernels  65.9 us (99%)
  between operations  0.8 us (1%)
    pallas_call x1, Pallas kernels, local(): pl.pallas_call(kernel, out_shape=tuple((pltpu.VMEM(r.shape, r.dtype) for...  65 us

profile of v5, /device:TPU:1, one launch (start us, length us, event | category | flops | bytes accessed | tf_op | source)
XLA Modules:
  0.0 66.7 jit_solution(11403863483853388642)
XLA Ops:
  0.6 65.0 %expand.1 = (bf16[1024,256]{1,0:T(8,128)(2,1)S(1)}, f32[32,1024]{1,0:T(8,128)S(1)}, f32[32,1024]{1,0:T(8,128)S(1)}) custom-call(bf16[1024,256]{1,0:T(8,128)(2,1)} %gal_far.1, s32[10,1024]{1,0:T(8,128)} %bitcast.2, bf16[128,256]{1,0:T(8,128)(2,1)} %q_far.1, s32[10,128]{1,0:T(8,128)} %bitcast.3), custom_call_target="tpu_custom_call" | custom-call | tf_op jit(solution)/shard_map/expand/pallas_call | solution.py:402
  65.6 0.9 %hand_over.1 = (bf16[1024,256]{1,0:T(8,128)(2,1)}, f32[32,1024]{1,0:T(8,128)}, f32[32,1024]{1,0:T(8,128)}) custom-call(bf16[1024,256]{1,0:T(8,128)(2,1)S(1)} %get-tuple-element.6.aug_in, f32[32,1024]{1,0:T(8,128)S(1)} %get-tuple-element.7.first_in, f32[32,1024]{1,0:T(8,128)S(1)} %get-tuple-element.8.final_in), custom_call_target="tpu_custom_call" | custom-call | tf_op jit(solution)/shard_map/hand_over/pallas_call | solution.py:453
